TPU v7x, 32 devices: a whole 2x2x4 slice. The times are simulated.
32 devices in a mesh: gx: 8 (over z, x), gy: 4 (over y, core).
Axes of the slice: x: 2, y: 2, z: 4, core: 2. Of those that a mesh axis runs over, the one named last changes fastest.
Arguments:
- control: float32 [2, 32, 256, 1024], P(None, None, 'gx', 'gy'), may hold values from -6 to 6
- band_roots: float32 [16, 32, 32], replicated, may hold values from -1 to 1
Outputs:
- increment: float32 [2, 32, 256, 1024], P(None, None, 'gx', 'gy')
All inputs are finite; a program needn't handle non-finite values.
Results may differ from a plain program's by a relative error of at most 0.000053.
Values sent between devices are 32-bit elements; how exact they have to be, the bound alone decides.
No kernel may reach another device: no remote copies, remote signals or barrier semaphores. Data moves between devices by JAX's collectives and lax.ppermute only.
A program may use at most 64 MiB of HBM per device.

v0:
```python
from functools import lru_cache, partial

import jax
import jax.numpy as jnp
import numpy as np
from jax import lax
from jax.experimental import pallas as pl
from jax.experimental.pallas import tpu as pltpu
from jax.sharding import PartitionSpec as P

LEVELS = 5
TILE = 128
VMEM_LIMIT = 28 * 2**20
BF = jnp.bfloat16
F32 = jnp.float32


def lift_np(signal):
    even, odd = signal[0::2], signal[1::2]
    zero = np.zeros_like(even[:1])
    detail = odd - 0.5 * (even + np.concatenate([even[1:], zero]))
    return even + 0.25 * (np.concatenate([zero, detail[:-1]]) + detail), detail


def unlift_np(smooth, detail):
    zero = np.zeros_like(smooth[:1])
    even = smooth - 0.25 * (np.concatenate([zero, detail[:-1]]) + detail)
    odd = detail + 0.5 * (even + np.concatenate([even[1:], zero]))
    return np.stack([even, odd], 1).reshape(2 * even.shape[0], -1)


def lane_plan(ny):
    place, lane = {}, 0
    spans = {}
    for k in list(range(3, LEVELS + 1)) + [1, 2]:
        n = ny >> k
        first = lane
        for kind, lo in (("s", 0), ("d", -1)):
            start = lane
            for i in range(lo, n + 1):
                if k <= 2 and 0 <= i < n:
                    place[k, kind, i] = (f"m{k}", i + (n if kind == "d" else 0))
                else:
                    place[k, kind, i] = ("c", lane)
                    lane += 1
            spans[k, kind] = (start, lane)
        spans[k] = (first, lane)
    assert lane <= TILE
    return place, spans


SLOT = 16


def edge_lanes(side):
    out = []
    for k in range(1, LEVELS + 1):
        if side > 0:
            out += [(k, "d", -1)] + ([(k, "d", 0), (k, "s", 0)] if k > 1 else [])
        else:
            out += [(k, "d", -1), (k, "d", 0), (k, "s", 0)]
    assert len(out) <= SLOT
    return out


@lru_cache(None)
def y_matrices(ny, below, above):
    place, _ = lane_plan(ny)
    off = ny if below else 0
    size = off + ny + (ny if above else 0)
    width = {"m1": ny, "m2": ny // 2, "c": TILE}
    ana = {a: np.zeros((ny, w)) for a, w in width.items()}
    syn = {a: np.zeros((w, ny)) for a, w in width.items()}
    send = {side: np.zeros((ny, SLOT)) for side in (1, -1)}
    s = np.eye(size)
    for k in range(1, LEVELS + 1):
        s, d = lift_np(s)
        for kind, mat in (("s", s), ("d", d)):
            n, o, own = size >> k, off >> k, ny >> k
            for side in (1, -1):
                for lane, (level, what, i) in enumerate(edge_lanes(side)):
                    at = o + i + (own if side > 0 else 0)
                    if (level, what) == (k, kind) and 0 <= at < n:
                        send[side][:, lane] = mat[at][off : off + ny]
            for i in range(0 if kind == "s" else -1, own + 1):
                if not 0 <= o + i < n:
                    continue
                arr, lane = place[k, kind, i]
                ana[arr][:, lane] = mat[o + i][off : off + ny]
                unit = np.zeros((n, 1))
                unit[o + i] = 1.0
                zero = np.zeros_like(unit)
                back = unlift_np(unit, zero) if kind == "s" else unlift_np(zero, unit)
                for _ in range(k - 1):
                    back = unlift_np(back, np.zeros_like(back))
                syn[arr][lane] = back[off : off + ny, 0]
    return ana, syn, send


@lru_cache(None)
def y_received(ny):
    place, _ = lane_plan(ny)
    base = {"m1": 0, "m2": ny, "c": ny + ny // 2}
    mat = np.zeros((2 * SLOT, base["c"] + TILE))

    def put(row, k, kind, i, value):
        arr, lane = place[k, kind, i]
        mat[row, base[arr] + lane] += value

    for row, (k, kind, i) in enumerate(edge_lanes(1)):
        put(row, k, kind, i, 1.0)
        if kind == "d" and i == (-1 if k == 1 else 0):
            put(row, k, "s", i + 1, 0.25)
    for row, (k, kind, i) in enumerate(edge_lanes(-1)):
        n = ny >> k
        put(SLOT + row, k, kind, n + i, 1.0)
        if kind == "d" and i == -1:
            put(SLOT + row, k, "s", n - 1, 0.25)
    groups = TILE // SLOT
    return np.concatenate([np.tile(mat[:SLOT], (groups, 1)), np.tile(mat[SLOT:], (groups, 1))], 0)


def split_np(mat):
    hi = mat.astype(np.float32).astype(jnp.bfloat16)
    lo = (mat - hi.astype(np.float64)).astype(np.float32).astype(jnp.bfloat16)
    return hi, lo


@lru_cache(None)
def y_constants(ny, count):
    if count == 1:
        kinds = [(False, False)]
    else:
        kinds = [(False, True), (True, True), (True, False)]
    main, e_hi, e_lo, back = [], [], [], []
    for below, above in kinds:
        ana, syn, send = y_matrices(ny, below, above)
        hi, lo = split_np(np.concatenate([ana["m1"], ana["m2"]], 1))
        assert not np.any(lo.astype(np.float32))
        main.append(hi)
        edge = np.tile(np.concatenate([send[1], send[-1]], 1), (1, TILE // (2 * SLOT)))
        hi, lo = split_np(np.concatenate([ana["c"], edge], 1))
        e_hi.append(hi)
        e_lo.append(lo)
        hi, lo = split_np(np.concatenate([syn["m1"], syn["m2"], syn["c"]], 0))
        assert not np.any(lo.astype(np.float32))
        back.append(hi)
    return np.stack(main), np.stack(e_hi), np.stack(e_lo), np.stack(back), split_np(y_received(ny))[0]


def split(value):
    hi = value.astype(BF)
    return hi, (value - hi.astype(F32)).astype(BF)


def dot(a, b):
    return jnp.dot(a, b, preferred_element_type=F32)


def lanes():
    return lax.broadcasted_iota(jnp.int32, (1, TILE), 1)


def in_span(span):
    lane = lanes()
    return (lane >= span[0]) & (lane < span[1])


def first_kernel(nx, edge_ref, var_ref, x_ref, ehi_ref, elo_ref, xhl, yc_ref, one_ref, two_ref, xt, e3, sems):
    g, ny = xt.shape[1], xt.shape[2]
    consts = [
        pltpu.make_async_copy(ref.at[var_ref[0]], e3.at[pl.ds(j * ny, ny)], sems.at[nx + j])
        for j, ref in enumerate((ehi_ref, ehi_ref, elo_ref))
    ]
    copies = [pltpu.make_async_copy(x_ref.at[:, i], xt.at[i], sems.at[i]) for i in range(nx)]
    for copy in copies[:4] + consts + copies[4:]:
        copy.start()
    per = TILE // SLOT
    odd = var_ref[1] == 1
    for r in range(0, nx, per):
        up = down = None
        for q in range(r, r + per, 4):
            for i in range(q, q + 4):
                copies[i].wait()
                rows = slice(i * g, (i + 1) * g)
                hi, lo = split(xt[i])
                xhl[rows, 0:ny], xhl[rows, ny : 2 * ny], xhl[rows, 2 * ny : 3 * ny] = hi, lo, hi
            if q == 0:
                for copy in consts:
                    copy.wait()
            res = dot(xhl[q * g : (q + 4) * g], e3[...])
            for i in range(q, q + 4):
                part = res[(i - q) * g : (i - q + 1) * g]
                yc_ref[i] = part[:, 0:TILE]
                plain = part[:, TILE : 2 * TILE]
                turned = pltpu.roll(plain, SLOT, 1)
                group = lanes() // SLOT == i - r
                a, b = (plain, turned) if i % 2 == 0 else (turned, plain)
                up = jnp.where(group, a, 0.0 if up is None else up)
                down = jnp.where(group, b, 0.0 if down is None else down)
        one_ref[r // per] = jnp.where(odd, down, up)
        two_ref[r // per] = jnp.where(odd, up, down)


def main_kernel(nx, edge_ref, var_ref, xhl, a_ref, y_ref, a2):
    g, ny = y_ref.shape[1], a_ref.shape[1]
    a2[0:ny], a2[ny : 2 * ny] = a_ref[0], a_ref[0]
    step = 4
    for r in range(0, nx, step):
        res = dot(xhl[r * g : (r + step) * g, 0 : 2 * ny], a2[...])
        y_ref[r : r + step] = res.reshape(step, g, res.shape[1])


class Lift:
    def __init__(self, nx, raw, edge_ref, first=0, last=None):
        self.nx, self.raw = nx, raw
        self.first, self.last = first, nx - 1 if last is None else last
        self.not_first, self.not_last = edge_ref[0], edge_ref[1]
        self.known = {}

    def smooth(self, k, i):
        if k == 0:
            if not 0 <= i < self.nx:
                return None
            assert self.first <= i <= self.last
        if (k, "s", i) not in self.known:
            self.known[k, "s", i] = self.raw(i) if k == 0 else self.new_smooth(k, i)
        return self.known[k, "s", i]

    def detail(self, k, i):
        if (k, "d", i) not in self.known:
            self.known[k, "d", i] = self.new_detail(k, i)
        return self.known[k, "d", i]

    def new_detail(self, k, i):
        if not -1 <= i <= self.nx >> k:
            return None
        even, mid, after = (self.smooth(k - 1, j) for j in (2 * i, 2 * i + 1, 2 * i + 2))
        pair = plus(even, after)
        if pair is None:
            return mid
        out = -0.5 * pair if mid is None else mid - 0.5 * pair
        return out * self.not_first if i < 0 else out

    def new_smooth(self, k, i):
        if not -1 <= i <= (self.nx >> k) + 1:
            return None
        even = self.smooth(k - 1, 2 * i)
        pair = plus(self.detail(k, i - 1), self.detail(k, i))
        if pair is None:
            return even if even is None or i < self.nx >> k else even * self.not_last
        out = 0.25 * pair if even is None else even + 0.25 * pair
        return out * self.not_last if i >= self.nx >> k else out


def plus(a, b):
    return b if a is None else a if b is None else a + b


def c_slots(lift, spans, kind, low, high, s_lanes):
    out = []
    for i in range(low, high + 1):
        tile = None
        for k in range(1, LEVELS + 1):
            if i > lift.nx >> k:
                continue
            value = lift.detail(k, i) if kind == "d" else lift.smooth(k, i)
            if value is None:
                continue
            tile = jnp.where(in_span(spans[k]), value, 0.0 if tile is None else tile)
        out.append(jnp.where(s_lanes, tile, 0.0) if kind == "s" else tile)
    return out


def smooth_lanes(spans):
    ok = in_span(spans[LEVELS])
    for k in range(1, LEVELS):
        ok = ok | in_span(spans[k, "d"])
    return ok


def send_kernel(nx, far, edge_ref, var_ref, yc_ref, ym_ref, one_ref, two_ref, p_ref, *rest):
    up_ref, down_ref, cc_ref, z = rest[:4]
    rest = rest[4:]
    if far:
        up2_ref, down2_ref = rest[:2]
        rest = rest[2:]
    yc, yl, yh, p2 = rest
    g = yc.shape[1]
    mains = ym_ref.shape[2]
    ny = mains - TILE
    half = ny // 2
    _, spans = lane_plan(ny)
    n1, n2 = nx >> 1, nx >> 2
    n = 2 * TILE
    p2[0:n], p2[n : 2 * n] = p_ref[...], p_ref[...]
    per = TILE // SLOT
    group = lanes() // SLOT
    zero = jnp.zeros((g, TILE), BF)
    odd = var_ref[1] == 1
    for t in range(nx // per):
        from_below = jnp.where(odd, one_ref[t], two_ref[t])
        from_above = jnp.where(odd, two_ref[t], one_ref[t])
        pieces = split(from_below) + split(from_above)
        for i in range(per):
            here = group == i
            rows = slice((t * per + i) * g, (t * per + i + 1) * g)
            for c, j in enumerate((0, 2, 1, 3)):
                z[rows, c * TILE : (c + 1) * TILE] = jnp.where(here, pieces[j], zero)
    step = 4
    for r in range(0, nx, step):
        res = dot(z[r * g : (r + step) * g], p2[:, mains : mains + TILE])
        yc[r : r + step] = yc_ref[r : r + step] + res.reshape(step, g, TILE)
    low, high = yl.shape[0], yh.shape[0]
    yl[...] = ym_ref[0:low] + dot(z[0 : low * g], p2[:, 0:mains]).reshape(yl.shape)
    yh[...] = ym_ref[nx - high :] + dot(z[(nx - high) * g :], p2[:, 0:mains]).reshape(yh.shape)

    def place(ref, tile, value):
        for t in range(value.shape[1] // TILE):
            ref[tile + t] = value[:, t * TILE : (t + 1) * TILE]

    m1, m1d, m2 = slice(0, ny), slice(half, ny), slice(ny, ny + half)

    def lift(ref, base, columns, first, last):
        return Lift(nx, lambda i: ref[i - base, :, columns], edge_ref, first, last)

    top = nx - high
    place(up_ref, 0, lift(yh, top, m1, top, nx - 1).detail(1, n1 - 1))
    one = lift(yh, top, m2, top, nx - 1)
    up_ref[2], up_ref[3], up_ref[4] = one.detail(2, n2 - 1), one.detail(2, n2), one.smooth(2, n2)
    one = lift(yl, 0, m1, 0, low - 1)
    place(down_ref, 0, one.detail(1, -1))
    place(down_ref, 2, one.detail(1, 0))
    down_ref[4] = lift(yl, 0, m1d, 0, low - 1).smooth(1, 0)
    one = lift(yl, 0, m2, 0, low - 1)
    down_ref[5], down_ref[6], down_ref[7] = one.detail(2, -1), one.detail(2, 0), one.smooth(2, 0)

    s_lanes = smooth_lanes(spans)
    deep = Lift(nx, lambda i: yc[i], edge_ref)
    for j, tile in enumerate(c_slots(deep, spans, "d", -1, n1 - 1, s_lanes)):
        cc_ref[j] = tile
    for j, tile in enumerate(c_slots(deep, spans, "s", 0, n1, s_lanes)):
        cc_ref[n1 + 1 + j] = tile
    acc = [jnp.zeros((g, TILE), F32)] * 3
    for k in range(1, LEVELS + 1):
        n, here = nx >> k, in_span(spans[k])
        new = [deep.detail(k, n - 1)] + ([deep.detail(k, n), deep.smooth(k, n)] if k > 1 else [None] * 2)
        acc = [a if v is None else jnp.where(here, v, a) for a, v in zip(acc, new)]
    for t in range(3):
        up_ref[5 + t] = acc[t]
    down_ref[8], down_ref[9], down_ref[10] = cc_ref[0], cc_ref[1], cc_ref[n1 + 1]
    if far:
        here = in_span(spans[LEVELS])
        up2_ref[...] = jnp.where(here, deep.detail(LEVELS, nx >> LEVELS), 0.0)
        down2_ref[...] = jnp.where(here, deep.detail(LEVELS, -1), 0.0)


def weigh(r_ref, bands, value):
    m = r_ref.shape[1]
    vectors = value.shape[0] // m
    hi, lo = split(value)
    out = [[] for _ in bands]
    mats = [r_ref[b] for b in bands]
    mat = mats[0] if len(mats) == 1 else jnp.concatenate(mats, 0)
    for v in range(vectors):
        part = slice(v * m, (v + 1) * m)
        rhs = jnp.concatenate([hi[part], hi[part], lo[part]], 0)
        res = dot(mat, rhs)
        for j in range(len(bands)):
            out[j].append(res[j * m : (j + 1) * m])
    return [jnp.concatenate(o, 0) for o in out]


def band_of(k, kind, y_kind):
    if kind == "s":
        return 3 * LEVELS if y_kind == "s" else 3 * (k - 1)
    return 3 * (k - 1) + (1 if y_kind == "s" else 2)


def weigh_c(r_ref, spans, kind, levels, tiles):
    which = [
        (k, y_kind)
        for k in levels
        for y_kind in ("s", "d")
        if kind == "d" or y_kind == "d" or k == LEVELS
    ]
    value = jnp.concatenate(tiles, 1) if len(tiles) > 1 else tiles[0]
    res = weigh(r_ref, [band_of(k, kind, y_kind) for k, y_kind in which], value)
    outs = []
    for t in range(len(tiles)):
        out = jnp.zeros_like(tiles[t])
        for (k, y_kind), r in zip(which, res):
            out = jnp.where(in_span(spans[k, y_kind]), r[:, t * TILE : (t + 1) * TILE], out)
        outs.append(out)
    return outs


def weigh_m2(r_ref, kind, tiles):
    lane_d = lanes() >= TILE // 2
    value = jnp.concatenate(tiles, 1) if len(tiles) > 1 else tiles[0]
    if kind == "s":
        res = [None, weigh(r_ref, [band_of(2, "s", "d")], value)[0]]
    else:
        res = weigh(r_ref, [band_of(2, "d", "s"), band_of(2, "d", "d")], value)
    outs = []
    for t in range(len(tiles)):
        a, b = (0.0 if r is None else r[:, t * TILE : (t + 1) * TILE] for r in res)
        outs.append(jnp.where(lane_d, b, a))
    return outs


def weigh_tiles(r_ref, band, tiles):
    value = jnp.concatenate(tiles, 1) if len(tiles) > 1 else tiles[0]
    res = weigh(r_ref, [band], value)[0]
    return [res[:, t * TILE : (t + 1) * TILE] for t in range(len(tiles))]


def groups(low, high, size):
    return [list(range(i, min(i + size, high + 1))) for i in range(low, high + 1, size)]


def weighted_plan(nx):
    n2 = nx >> 2
    plan, at = {}, 0
    for name, count in ((("m2", "d"), n2 + 2), (("m2", "s"), n2 + 1), (("c", "d"), n2 + 2), (("c", "s"), n2 + 1)):
        plan[name] = at
        at += count
    return plan, at


def pairs_into(ref, row, g, tiles):
    rows, width = slice(row * g, (row + 1) * g), len(tiles) * TILE
    for t, tile in enumerate(tiles):
        if tile is None:
            continue
        cols = slice(t * TILE, (t + 1) * TILE)
        ref[rows, cols], ref[rows, width + t * TILE : width + (t + 1) * TILE] = split(tile)


def stack_back(s_ref, out, spans_of_rows):
    at = 0
    for a, b in spans_of_rows * 2:
        out[at : at + b - a] = s_ref[0, a:b]
        at += b - a


def first_level_rows(ny):
    half, c = ny // 2, (ny + ny // 2, ny + ny // 2 + TILE)
    return [(0, ny), c], [(half, ny), c]


def local_kernel(nx, edge_ref, var_ref, ym_ref, z, cc_ref, p_ref, s_ref, r_ref,
                 vd_ref, vs_ref, w_ref, y, p2, zd, zs, sd, ss):
    g, mains = y.shape[1], y.shape[2]
    ny = mains - TILE
    _, spans = lane_plan(ny)
    n1, n2 = nx >> 1, nx >> 2
    plan, _ = weighted_plan(nx)
    n = 2 * TILE
    p2[0:n], p2[n : 2 * n] = p_ref[:, 0:mains], p_ref[:, 0:mains]
    rows_d, rows_s = first_level_rows(ny)
    stack_back(s_ref, sd, rows_d)
    stack_back(s_ref, ss, rows_s)
    step = 4
    for r in range(0, nx, step):
        res = dot(z[r * g : (r + step) * g], p2[...])
        y[r : r + step] = ym_ref[r : r + step] + res.reshape(step, g, mains)

    def lift(columns):
        return Lift(nx, lambda i: y[i, :, columns], edge_ref)

    a, b, m2 = (lift(slice(t * TILE, (t + 1) * TILE)) for t in range(3))

    def store(name, low, some, tiles):
        for i, tile in zip(some, tiles):
            w_ref[plan[name] + i - low] = tile

    here = in_span(spans[1])

    def weighed_c(kind, low, some):
        base = 0 if kind == "d" else n1 + 1
        out = {}
        by_levels = {}
        for i in some:
            by_levels.setdefault(tuple(k for k in range(1, LEVELS + 1) if i <= nx >> k), []).append(i)
        for levels, part in by_levels.items():
            tiles = weigh_c(r_ref, spans, kind, list(levels), [cc_ref[base + i - low] for i in part])
            for i, tile in zip(part, tiles):
                if i <= n2:
                    w_ref[plan["c", kind] + i - low] = tile
                out[i] = jnp.where(here, tile, 0.0) if i <= n2 else tile
        return [out[i] for i in some]

    for some in groups(-1, n1 - 1, 4):
        ta = weigh_tiles(r_ref, band_of(1, "d", "s"), [a.detail(1, i) for i in some])
        tb = weigh_tiles(r_ref, band_of(1, "d", "d"), [b.detail(1, i) for i in some])
        tc = weighed_c("d", -1, some)
        for i, tiles in zip(some, zip(ta, tb, tc)):
            pairs_into(zd, i + 1, g, tiles)
        first, count = some[0] + 1, len(some)
        vd_ref[first : first + count] = dot(zd[first * g : (first + count) * g], sd[...]).reshape(count, g, ny)
    for some in groups(0, n1, 4):
        tb = weigh_tiles(r_ref, band_of(1, "s", "d"), [b.smooth(1, i) for i in some])
        tc = weighed_c("s", 0, some)
        for i, tiles in zip(some, zip(tb, tc)):
            pairs_into(zs, i, g, tiles)
        first, count = some[0], len(some)
        vs_ref[first : first + count] = dot(zs[first * g : (first + count) * g], ss[...]).reshape(count, g, ny)
    for some in groups(-1, n2, 4):
        store(("m2", "d"), -1, some, weigh_m2(r_ref, "d", [m2.detail(2, i) for i in some]))
    for some in groups(0, n2, 4):
        store(("m2", "s"), 0, some, weigh_m2(r_ref, "s", [m2.smooth(2, i) for i in some]))


def final_kernel(nx, far, edge_ref, var_ref, vd_ref, vs_ref, w_ref, up_ref, down_ref, *rest):
    if far:
        up2_ref, down2_ref = rest[:2]
        rest = rest[2:]
    s_ref, r_ref, out_ref, sd, ss, sdeep, zd, zs, zdeep, rows, ot, sem = rest
    g, ny = ot.shape[1], ot.shape[2]
    _, spans = lane_plan(ny)
    plan, _ = weighted_plan(nx)
    half = ny // 2
    n1, n2 = nx >> 1, nx >> 2
    rows_d, rows_s = first_level_rows(ny)
    stack_back(s_ref, sd, rows_d)
    stack_back(s_ref, ss, rows_s)
    stack_back(s_ref, sdeep, [(ny, ny + half + TILE)])
    s_lanes = smooth_lanes(spans)
    lev1 = in_span(spans[1])

    def smooth_c(value):
        return jnp.where(s_lanes, 0.25 * value, 0.0)

    c_d = {-1: up_ref[5], 0: up_ref[6], "n-1": down_ref[8], "n": down_ref[9]}
    c_s = {
        0: up_ref[7] + jnp.where(lev1, smooth_c(c_d[-1]), 0.0),
        1: smooth_c(c_d[0]),
        "n-1": smooth_c(c_d["n-1"]),
        "n": down_ref[10],
    }
    if far:
        c_d[-1] = c_d[-1] + up2_ref[...]
        c_s[0] = c_s[0] + smooth_c(up2_ref[...])
        c_d["n"] = c_d["n"] + down2_ref[...]
        c_s["n"] = c_s["n"] + smooth_c(down2_ref[...])
    every = list(range(1, LEVELS + 1))
    got = {}

    def keep(name, keys, tiles):
        for key, tile in zip(keys, tiles):
            got[name, key] = tile

    for kind, tiles in (("d", c_d), ("s", c_s)):
        keep(("c", kind), list(tiles), weigh_c(r_ref, spans, kind, every, list(tiles.values())))
    keys = [-1, "n-1", "n"]
    ta = weigh_tiles(r_ref, band_of(1, "d", "s"), [up_ref[0], down_ref[0], down_ref[2]])
    tb = weigh_tiles(r_ref, band_of(1, "d", "d"), [up_ref[1], down_ref[1], down_ref[3]])
    for j, key in enumerate(keys):
        pairs_into(zd, j, g, [ta[j], tb[j], jnp.where(lev1, got[("c", "d"), key], 0.0)])
    more_d = dot(zd[...], sd[...])
    tb = weigh_tiles(r_ref, band_of(1, "s", "d"), [0.25 * up_ref[1], 0.25 * down_ref[1], down_ref[4]])
    for j, key in enumerate([0, "n-1", "n"]):
        pairs_into(zs, j, g, [tb[j], jnp.where(lev1, got[("c", "s"), key], 0.0)])
    more_s = dot(zs[...], ss[...])
    keep(("m2", "d"), [-1, 0, "n-1", "n"], weigh_m2(r_ref, "d", [up_ref[2], up_ref[3], down_ref[5], down_ref[6]]))
    keep(("m2", "s"), [0, 1, "n-1", "n"],
         weigh_m2(r_ref, "s", [up_ref[4], 0.25 * up_ref[3], 0.25 * down_ref[5], down_ref[7]]))

    def value_of(array, kind, k, i):
        n, low = nx >> k, -1 if kind == "d" else 0
        v = w_ref[plan[array, kind] + i - low]
        for key, at in ((-1, -1), (0, 0), (1, 1), ("n-1", n - 1), ("n", n)):
            if at == i and ((array, kind), key) in got:
                v = v + got[(array, kind), key]
        return jnp.where(in_span(spans[k]), v, 0.0) if array == "c" else v

    not_last = edge_ref[1]

    def unlift(n, smooth, detail, emit):
        below, before = detail(-1), None
        for i in range(n + 1):
            here = detail(i)
            even = smooth(i) - 0.25 * (below + here)
            if i == n:
                even = even * not_last
            if i > 0:
                emit(2 * i - 1, below + 0.5 * (before + even))
            emit(2 * i, even)
            below, before = here, even

    for k in range(LEVELS, 1, -1):
        base = level_base(nx, k)

        def smooth_deep(i, k=k, base=base):
            v = value_of("c", "s", k, i)
            return v if k == LEVELS else v + rows[base + i]

        if k > 2:
            def emit(i, value, base=level_base(nx, k - 1)):
                rows[base + i] = value
        else:
            def emit(i, value):
                r = slice(i * g, (i + 1) * g)
                zdeep[r, TILE : 2 * TILE], zdeep[r, 3 * TILE : 4 * TILE] = split(value)

        unlift(nx >> k, smooth_deep, lambda i, k=k: value_of("c", "d", k, i), emit)

    def emit_m2(i, value):
        r = slice(i * g, (i + 1) * g)
        zdeep[r, 0:TILE], zdeep[r, 2 * TILE : 3 * TILE] = split(value)

    unlift(n2, lambda i: value_of("m2", "s", 2, i), lambda i: value_of("m2", "d", 2, i), emit_m2)

    extra_d = {-1: more_d[0:g], n1 - 1: more_d[g : 2 * g], n1: more_d[2 * g :]}
    extra_s = {0: more_s[0:g], n1 - 1: more_s[g : 2 * g], n1: more_s[2 * g :]}
    step = 4
    deep = {}

    def smooth_first(i):
        if i % step == 0:
            count = min(step, n1 + 1 - i)
            res = dot(zdeep[i * g : (i + count) * g], sdeep[...])
            for j in range(count):
                deep[i + j] = res[j * g : (j + 1) * g]
        v = deep[i] + vs_ref[i]
        return v + extra_s[i] if i in extra_s else v

    def detail_first(i):
        if i == n1:
            return extra_d[i]
        v = vd_ref[i + 1]
        return v + extra_d[i] if i in extra_d else v

    copies = []

    def emit_out(i, value):
        if i < nx:
            ot[i] = value
            copies.append(pltpu.make_async_copy(ot.at[i], out_ref.at[:, i], sem.at[i]))
            copies[-1].start()

    unlift(n1, smooth_first, detail_first, emit_out)
    for copy in copies:
        copy.wait()


def level_base(nx, k):
    return sum((nx >> j) + 1 for j in range(max(k + 1, 3), LEVELS)) if k > 1 else 0


def shift(value, axis, step):
    count = lax.axis_size(axis)
    pairs = [(i, i + step) for i in range(count) if 0 <= i + step < count]
    return lax.ppermute(value, axis, pairs)


def swap(value, axis, first):
    count = lax.axis_size(axis)
    starts = range(first, count - 1, 2)
    return lax.ppermute(value, axis, [p for i in starts for p in ((i, i + 1), (i + 1, i))])


def per_device(control, band_roots):
    vectors, m, nx, ny = control.shape
    g = vectors * m
    half = ny // 2
    gx, gy = lax.axis_size("gx"), lax.axis_size("gy")
    per = TILE // SLOT
    assert half == TILE and nx % (2 * per) == 0
    far = (nx >> LEVELS) < 2 and gx > 2
    consts = y_constants(ny, gy)
    main_mat, ehi_mat, elo_mat, s_mat, p_mat = (jnp.asarray(t) for t in consts)
    n1, n2 = nx >> 1, nx >> 2
    mains = ny + half

    ix, iy = lax.axis_index("gx"), lax.axis_index("gy")
    edge = jnp.stack([ix > 0, ix < gx - 1]).astype(F32)
    which = jnp.where(iy == 0, 0, jnp.where(iy == gy - 1, 2, 1)) if gy > 1 else jnp.zeros((), jnp.int32)
    which = jnp.stack([which, iy % 2, ix % 2]).astype(jnp.int32)
    r_hi = lax.reduce_precision(band_roots, 8, 7)
    r_lo = band_roots - r_hi
    roots = jnp.concatenate([r_hi.astype(BF), r_lo.astype(BF), r_hi.astype(BF)], 2)

    hbm = pl.BlockSpec(memory_space=pl.ANY)
    vmem = pl.BlockSpec(memory_space=pltpu.VMEM)

    def variant(mat):
        shape = (1,) + mat.shape[1:]
        return mat, pl.BlockSpec(shape, lambda i, e, v: (v[0], 0, 0))

    def call(kernel, ins, outs, scratches, name, out_specs=None):
        return pl.pallas_call(
            kernel,
            out_shape=tuple(jax.ShapeDtypeStruct(*s) for s in outs),
            grid_spec=pltpu.PrefetchScalarGridSpec(
                num_scalar_prefetch=2,
                grid=(1,),
                in_specs=[s for _, s in ins],
                out_specs=out_specs or (vmem,) * len(outs),
                scratch_shapes=scratches,
            ),
            name=name,
            compiler_params=pltpu.CompilerParams(vmem_limit_bytes=VMEM_LIMIT),
        )(edge, which, *[a for a, _ in ins])

    tile = (g, TILE)
    rows3 = control.reshape(g, nx, ny)
    far_hbm = pl.BlockSpec(memory_space=pltpu.HBM)
    xhl, yc, one, two = call(
        partial(first_kernel, nx),
        [(pltpu.with_memory_space_constraint(t, pltpu.HBM), far_hbm) for t in (rows3, ehi_mat, elo_mat)],
        [((nx * g, 3 * ny), BF), ((nx,) + tile, F32), ((nx // per,) + tile, F32), ((nx // per,) + tile, F32)],
        [pltpu.VMEM((nx, g, ny), F32), pltpu.VMEM((3 * ny, 2 * TILE), BF), pltpu.SemaphoreType.DMA((nx + 3,))],
        "first",
    )
    got_one = swap(one, "gy", 0)
    got_two = swap(two, "gy", 1)
    (ym,) = call(
        partial(main_kernel, nx),
        [(xhl, vmem), variant(main_mat)],
        [((nx, g, mains), F32)],
        [pltpu.VMEM((2 * ny, mains), BF)],
        "main",
    )
    slots = 2 * n1 + 2
    sent = call(
        partial(send_kernel, nx, far),
        [(yc, vmem), (ym, vmem), (got_one, vmem), (got_two, vmem), (p_mat, vmem)],
        [((8,) + tile, F32), ((11,) + tile, F32), ((slots,) + tile, F32), ((nx * g, 4 * TILE), BF)]
        + ([(tile, F32), (tile, F32)] if far else []),
        [
            pltpu.VMEM((nx,) + tile, F32),
            pltpu.VMEM((8, g, mains), F32),
            pltpu.VMEM((8, g, mains), F32),
            pltpu.VMEM((4 * TILE, mains + TILE), BF),
        ],
        "send",
    )
    got = [(shift(sent[0], "gx", 1), vmem), (shift(sent[1], "gx", -1), vmem)]
    if far:
        got += [(shift(sent[4], "gx", 2), vmem), (shift(sent[5], "gx", -2), vmem)]

    _, count = weighted_plan(nx)
    vd, vs, w = call(
        partial(local_kernel, nx),
        [(ym, vmem), (sent[3], vmem), (sent[2], vmem), (p_mat, vmem), variant(s_mat), (roots, vmem)],
        [((n1 + 1, g, ny), F32), ((n1 + 1, g, ny), F32), ((count,) + tile, F32)],
        [
            pltpu.VMEM((nx, g, mains), F32),
            pltpu.VMEM((4 * TILE, mains), BF),
            pltpu.VMEM(((n1 + 1) * g, 6 * TILE), BF),
            pltpu.VMEM(((n1 + 1) * g, 4 * TILE), BF),
            pltpu.VMEM((6 * TILE, ny), BF),
            pltpu.VMEM((4 * TILE, ny), BF),
        ],
        "local",
    )
    (out,) = call(
        partial(final_kernel, nx, far),
        [(vd, vmem), (vs, vmem), (w, vmem)] + got + [variant(s_mat), (roots, vmem)],
        [((g, nx, ny), F32)],
        [
            pltpu.VMEM((6 * TILE, ny), BF),
            pltpu.VMEM((4 * TILE, ny), BF),
            pltpu.VMEM((4 * TILE, ny), BF),
            pltpu.VMEM((3 * g, 6 * TILE), BF),
            pltpu.VMEM((3 * g, 4 * TILE), BF),
            pltpu.VMEM(((n1 + 1) * g, 4 * TILE), BF),
            pltpu.VMEM((level_base(nx, 1) + sum((nx >> j) + 1 for j in range(2, LEVELS)),) + tile, F32),
            pltpu.VMEM((nx, g, ny), F32),
            pltpu.SemaphoreType.DMA((nx,)),
        ],
        "final",
        (hbm,),
    )
    return out.reshape(control.shape)


def solution(mesh):
    in_specs = (P(None, None, "gx", "gy"), P())
    out_specs = P(None, None, "gx", "gy")
    return jax.shard_map(
        per_device, mesh=mesh, in_specs=in_specs, out_specs=out_specs, check_vma=False
    )
```

profile of v0, /device:TPU:19, one launch (start us, length us, event | category | flops | bytes accessed | tf_op | source)
XLA Modules:
  0.0 34.6 jit_solution(7664314321991847799)
XLA Ops:
  0.0 0.0 copy-start.2
  0.0 0.1 add_convert_fusion.edge_ref
  0.1 0.1 pad_add_fusion.var_ref
  0.2 5.7 %first.1 = (bf16[2048,768]{1,0:T(8,128)(2,1)S(1)}, f32[32,64,128]{2,1,0:T(8,128)S(1)}, f32[4,64,128]{2,1,0:T(8,128)S(1)}, f32[4,64,128]{2,1,0:T(8,128)S(1)}) custom-call(f32[2]{0:T(128)S(1)} %add_convert_fusion.edge_ref, s32[3]{0:T(128)S(1)} %pad_add_fusion.var_ref, f32[64,32,256]{2,1,0:T(8,128)} %bitcast.7, bf16[3,256,256]{2,1,0:T(8,128)(2,1)} %constant.43.clone.ehi_ref, ...), custom_call_target="tpu_custom_call" | custom-call | tf_op jit(solution)/shard_map/first/pallas_call | solution.py:693
  5.8 0.7 %collective-permute-start = (f32[4,64,128]{2,1,0:T(8,128)S(1)}, f32[4,64,128]{2,1,0:T(8,128)S(1)}, u32[]{:S(2)}, u32[]{:S(2)}) collective-permute-start(f32[4,64,128]{2,1,0:T(8,128)S(1)} %get-tuple-element.20), channel_id=1, source_target_pairs={{0,1},{1,0},{2,3},{3,2},{4,5},{5,4},{6,7},{7,6},{8,9},{9,8},{10,11... | collective-permute-start | bytes 393224 | tf_op jit(solution)/shard_map/ppermute | solution.py:661
  6.6 3.0 %collective-permute-start.1 = (f32[4,64,128]{2,1,0:T(8,128)S(1)}, f32[4,64,128]{2,1,0:T(8,128)S(1)}, u32[]{:S(2)}, u32[]{:S(2)}) collective-permute-start(f32[4,64,128]{2,1,0:T(8,128)S(1)} %get-tuple-element.21), channel_id=1, source_target_pairs={{1,2},{2,1},{5,6},{6,5},{9,10},{10,9},{13,14},{14,13},{17,18},{18,... | collective-permute-start | bytes 393224 | tf_op jit(solution)/shard_map/ppermute | solution.py:661
  9.6 0.0 copy-done.2
  9.6 0.0 copy-start.1
  9.7 1.8 %main.1.ym_ref = f32[32,64,384]{2,1,0:T(8,128)S(1)} custom-call(f32[2]{0:T(128)S(1)} %add_convert_fusion.edge_ref, s32[3]{0:T(128)S(1)} %pad_add_fusion.var_ref, bf16[2048,768]{1,0:T(8,128)(2,1)S(1)} %get-tuple-element.18.xhl, bf16[3,256,384]{2,1,0:T(8,128)(2,1)S(1)} %copy-done.2), custom_call_target="tpu_custom_call" | custom-call | tf_op jit(solution)/shard_map/main/pallas_call | solution.py:693
  11.5 0.0 collective-permute-done.one_ref
  11.5 1.4 %collective-permute-done.1.two_ref = f32[4,64,128]{2,1,0:T(8,128)S(1)} collective-permute-done((f32[4,64,128]{2,1,0:T(8,128)S(1)}, f32[4,64,128]{2,1,0:T(8,128)S(1)}, u32[]{:S(2)}, u32[]{:S(2)}) %collective-permute-start.1) | collective-permute-done | bytes 131104 | tf_op jit(solution)/shard_map/ppermute | solution.py:661
  12.9 0.0 copy-done.1
  12.9 0.0 copy-start.3
  12.9 0.0 copy-start
  12.9 2.1 %send.1 = (f32[8,64,128]{2,1,0:T(8,128)S(1)}, f32[11,64,128]{2,1,0:T(8,128)S(1)}, f32[34,64,128]{2,1,0:T(8,128)S(1)}, bf16[2048,512]{1,0:T(8,128)(2,1)S(1)}, f32...) custom-call(f32[2]{0:T(128)S(1)} %add_convert_fusion.edge_ref, s32[3]{0:T(128)S(1)} %pad_add_fusion.var_ref, ...), custom_call_target="tpu_custom_call" | custom-call | tf_op jit(solution)/shard_map/send/pallas_call | solution.py:693
  15.0 2.2 %collective-permute-start.3 = (f32[11,64,128]{2,1,0:T(8,128)S(1)}, f32[11,64,128]{2,1,0:T(8,128)S(1)}, u32[]{:S(2)}, u32[]{:S(2)}) collective-permute-start(f32[11,64,128]{2,1,0:T(8,128)S(1)} %get-tuple-element.28), channel_id=1, source_target_pairs={{4,0},{8,4},{12,8},{16,12},{20,16},{24,20},{28,24},{5,1},{9,5},{13... | collective-permute-start | bytes 1081352 | tf_op jit(solution)/shard_map/ppermute | solution.py:655
  17.1 4.0 %collective-permute-start.2 = (f32[8,64,128]{2,1,0:T(8,128)S(1)}, f32[8,64,128]{2,1,0:T(8,128)S(1)}, u32[]{:S(2)}, u32[]{:S(2)}) collective-permute-start(f32[8,64,128]{2,1,0:T(8,128)S(1)} %get-tuple-element.27), channel_id=1, source_target_pairs={{0,4},{4,8},{8,12},{12,16},{16,20},{20,24},{24,28},{1,5},{5,9},{9,... | collective-permute-start | bytes 786440 | tf_op jit(solution)/shard_map/ppermute | solution.py:655
  21.2 0.0 copy-done.3
  21.2 1.9 %collective-permute-start.4 = (f32[64,128]{1,0:T(8,128)S(1)}, f32[64,128]{1,0:T(8,128)S(1)}, u32[]{:S(2)}, u32[]{:S(2)}) collective-permute-start(f32[64,128]{1,0:T(8,128)S(1)} %get-tuple-element.29), channel_id=1, source_target_pairs={{0,8},{4,12},{8,16},{12,20},{16,24},{20,28},{1,9},{5,13},{9,17},{1... | collective-permute-start | bytes 98312 | tf_op jit(solution)/shard_map/ppermute | solution.py:655
  23.2 3.4 %collective-permute-start.5 = (f32[64,128]{1,0:T(8,128)S(1)}, f32[64,128]{1,0:T(8,128)S(1)}, u32[]{:S(2)}, u32[]{:S(2)}) collective-permute-start(f32[64,128]{1,0:T(8,128)S(1)} %get-tuple-element.30), channel_id=1, source_target_pairs={{8,0},{12,4},{16,8},{20,12},{24,16},{28,20},{9,1},{13,5},{17,9},{2... | collective-permute-start | bytes 98312 | tf_op jit(solution)/shard_map/ppermute | solution.py:655
  26.5 0.1 pad_maximum_fusion.r_ref.rest_3_
  26.7 0.0 copy-done
  26.7 4.1 %local.1 = (f32[17,64,256]{2,1,0:T(8,128)S(1)}, f32[17,64,256]{2,1,0:T(8,128)S(1)}, f32[38,64,128]{2,1,0:T(8,128)S(1)}) custom-call(f32[2]{0:T(128)S(1)} %add_convert_fusion.edge_ref, s32[3]{0:T(128)S(1)} %pad_add_fusion.var_ref, f32[32,64,384]{2,1,0:T(8,128)S(1)} %main.1.ym_ref, bf16[2048,512]{1,0:T(8,128)(2,1)S(1)} %get-tuple-element.22.z, ...), custom_call_target="tpu_custom_call" | custom-call | tf_op jit(solution)/shard_map/local/pallas_call | solution.py:693
  30.8 0.0 collective-permute-done.4.rest_0_
  30.8 0.0 collective-permute-done.5.rest_1_
  30.8 0.0 collective-permute-done.2.up_ref
  30.8 0.0 collective-permute-done.3.down_ref
  30.8 3.8 %final.1 = f32[64,32,256]{2,1,0:T(8,128)} custom-call(f32[2]{0:T(128)S(1)} %add_convert_fusion.edge_ref, s32[3]{0:T(128)S(1)} %pad_add_fusion.var_ref, f32[17,64,256]{2,1,0:T(8,128)S(1)} %get-tuple-element.24.vd_ref, f32[17,64,256]{2,1,0:T(8,128)S(1)} %get-tuple-element.25.vs_ref, f32[38,64,128]{2,1,0:T(8,128)S(1)} %get-tuple-element.26.w_ref, ...), custom_call_target="tpu_custom_call" | custom-call | tf_op jit(solution)/shard_map/final/pallas_call | solution.py:693
  (1 shorter events, 0.0 us)
Async XLA Ops:
  0.0 9.6 %copy-start.2 = (bf16[3,256,384]{2,1,0:T(8,128)(2,1)S(1)}, bf16[3,256,384]{2,1,0:T(8,128)(2,1)}, u32[]{:S(2)}) copy-start(bf16[3,256,384]{2,1,0:T(8,128)(2,1)} %constant.42.clone.a_ref) | copy-start | bytes 1769476
  5.8 5.7 %collective-permute-start = (f32[4,64,128]{2,1,0:T(8,128)S(1)}, f32[4,64,128]{2,1,0:T(8,128)S(1)}, u32[]{:S(2)}, u32[]{:S(2)}) collective-permute-start(f32[4,64,128]{2,1,0:T(8,128)S(1)} %get-tuple-element.20), channel_id=1, source_target_pairs={{0,1},{1,0},{2,3},{3,2},{4,5},{5,4},{6,7},{7,6},{8,9},{9,8},{10,11... | collective-permute-start | bytes 393224 | tf_op jit(solution)/shard_map/ppermute | solution.py:661
  6.6 6.3 %collective-permute-start.1 = (f32[4,64,128]{2,1,0:T(8,128)S(1)}, f32[4,64,128]{2,1,0:T(8,128)S(1)}, u32[]{:S(2)}, u32[]{:S(2)}) collective-permute-start(f32[4,64,128]{2,1,0:T(8,128)S(1)} %get-tuple-element.21), channel_id=1, source_target_pairs={{1,2},{2,1},{5,6},{6,5},{9,10},{10,9},{13,14},{14,13},{17,18},{18,... | collective-permute-start | bytes 393224 | tf_op jit(solution)/shard_map/ppermute | solution.py:661
  9.6 3.2 %copy-start.1 = (bf16[256,512]{1,0:T(8,128)(2,1)S(1)}, bf16[256,512]{1,0:T(8,128)(2,1)}, u32[]{:S(2)}) copy-start(bf16[256,512]{1,0:T(8,128)(2,1)} %constant.46.clone.p_ref) | copy-start | bytes 786436
  12.9 8.3 %copy-start.3 = (f32[16,32,32]{2,1,0:T(8,128)S(1)}, f32[16,32,32]{2,1,0:T(8,128)}, u32[]{:S(2)}) copy-start(f32[16,32,32]{2,1,0:T(8,128)} %param.8) | copy-start | bytes 196612
  12.9 13.8 %copy-start = (bf16[3,512,256]{2,1,0:T(8,128)(2,1)S(1)}, bf16[3,512,256]{2,1,0:T(8,128)(2,1)}, u32[]{:S(2)}) copy-start(bf16[3,512,256]{2,1,0:T(8,128)(2,1)} %constant.45.clone.s_ref.rest_2_) | copy-start | bytes 2359300
  15.0 15.8 %collective-permute-start.3 = (f32[11,64,128]{2,1,0:T(8,128)S(1)}, f32[11,64,128]{2,1,0:T(8,128)S(1)}, u32[]{:S(2)}, u32[]{:S(2)}) collective-permute-start(f32[11,64,128]{2,1,0:T(8,128)S(1)} %get-tuple-element.28), channel_id=1, source_target_pairs={{4,0},{8,4},{12,8},{16,12},{20,16},{24,20},{28,24},{5,1},{9,5},{13... | collective-permute-start | bytes 1081352 | tf_op jit(solution)/shard_map/ppermute | solution.py:655
  17.1 13.6 %collective-permute-start.2 = (f32[8,64,128]{2,1,0:T(8,128)S(1)}, f32[8,64,128]{2,1,0:T(8,128)S(1)}, u32[]{:S(2)}, u32[]{:S(2)}) collective-permute-start(f32[8,64,128]{2,1,0:T(8,128)S(1)} %get-tuple-element.27), channel_id=1, source_target_pairs={{0,4},{4,8},{8,12},{12,16},{16,20},{20,24},{24,28},{1,5},{5,9},{9,... | collective-permute-start | bytes 786440 | tf_op jit(solution)/shard_map/ppermute | solution.py:655
  21.2 9.5 %collective-permute-start.4 = (f32[64,128]{1,0:T(8,128)S(1)}, f32[64,128]{1,0:T(8,128)S(1)}, u32[]{:S(2)}, u32[]{:S(2)}) collective-permute-start(f32[64,128]{1,0:T(8,128)S(1)} %get-tuple-element.29), channel_id=1, source_target_pairs={{0,8},{4,12},{8,16},{12,20},{16,24},{20,28},{1,9},{5,13},{9,17},{1... | collective-permute-start | bytes 98312 | tf_op jit(solution)/shard_map/ppermute | solution.py:655
  23.2 7.6 %collective-permute-start.5 = (f32[64,128]{1,0:T(8,128)S(1)}, f32[64,128]{1,0:T(8,128)S(1)}, u32[]{:S(2)}, u32[]{:S(2)}) collective-permute-start(f32[64,128]{1,0:T(8,128)S(1)} %get-tuple-element.30), channel_id=1, source_target_pairs={{8,0},{12,4},{16,8},{20,12},{24,16},{28,20},{9,1},{13,5},{17,9},{2... | collective-permute-start | bytes 98312 | tf_op jit(solution)/shard_map/ppermute | solution.py:655
where the time goes:
time: 35.3 us; the launch traced here: 34.6 us
  Pallas kernels  17.5 us (50%)
  starting transfers between devices  15.2 us (43%)
  waiting for transfers between devices  1.36 us (4%)
    pallas_call x5, Pallas kernels, call(): pl.pallas_call(kernel, out_shape=tuple((jax.ShapeDtypeStruct(*s) for s in...  17.5 us
    ppermute x4, starting transfers between devices, shift(): return lax.ppermute(value, axis, pairs)  11.5 us
    ppermute x2, starting transfers between devices, swap(): lax.ppermute(value, axis, [p for i in starts for p in ((i, i + 1), (i + 1...  3.79 us
    ppermute x2, waiting for transfers between devices, swap(): lax.ppermute(value, axis, [p for i in starts for p in ((i, i + 1), (i + 1...  1.35 us
  transfers between devices with their start and end apart: 6, of which 1 were waited for; matrix products, arithmetic and copies ran while one was open for 1% of the time, Pallas kernels for 17%

commit v1 on v0

--- a/solution.py
+++ b/solution.py
@@ -135,7 +135,7 @@
     main, e_hi, e_lo, back = [], [], [], []
     for below, above in kinds:
         ana, syn, send = y_matrices(ny, below, above)
-        hi, lo = split_np(np.concatenate([ana["m1"], ana["m2"]], 1))
+        hi, lo = split_np(np.concatenate([ana["m1"], ana["m2"], np.zeros((ny, TILE))], 1))
         assert not np.any(lo.astype(np.float32))
         main.append(hi)
         edge = np.tile(np.concatenate([send[1], send[-1]], 1), (1, TILE // (2 * SLOT)))
@@ -167,23 +167,27 @@
 
 
 def first_kernel(nx, edge_ref, var_ref, x_ref, ehi_ref, elo_ref, xhl, yc_ref, one_ref, two_ref, xt, e3, sems):
-    g, ny = xt.shape[1], xt.shape[2]
+    g, ny = xt.shape[1], xt.shape[3]
     consts = [
         pltpu.make_async_copy(ref.at[var_ref[0]], e3.at[pl.ds(j * ny, ny)], sems.at[nx + j])
         for j, ref in enumerate((ehi_ref, ehi_ref, elo_ref))
     ]
-    copies = [pltpu.make_async_copy(x_ref.at[:, i], xt.at[i], sems.at[i]) for i in range(nx)]
-    for copy in copies[:4] + consts + copies[4:]:
+    per = TILE // SLOT
+    copies = [
+        pltpu.make_async_copy(x_ref.at[:, pl.ds(r, per)], xt.at[r // per], sems.at[r // per])
+        for r in range(0, nx, per)
+    ]
+    for copy in copies[:1] + consts + copies[1:]:
         copy.start()
-    per = TILE // SLOT
     odd = var_ref[1] == 1
     for r in range(0, nx, per):
         up = down = None
+        copies[r // per].wait()
+        block = jnp.swapaxes(xt[r // per], 0, 1)
         for q in range(r, r + per, 4):
             for i in range(q, q + 4):
-                copies[i].wait()
                 rows = slice(i * g, (i + 1) * g)
-                hi, lo = split(xt[i])
+                hi, lo = split(block[i - r])
                 xhl[rows, 0:ny], xhl[rows, ny : 2 * ny], xhl[rows, 2 * ny : 3 * ny] = hi, lo, hi
             if q == 0:
                 for copy in consts:
@@ -202,13 +206,33 @@
         two_ref[r // per] = jnp.where(odd, up, down)
 
 
-def main_kernel(nx, edge_ref, var_ref, xhl, a_ref, y_ref, a2):
+def main_kernel(nx, edge_ref, var_ref, xhl, a_ref, y_ref, one_ref, two_ref, a2):
     g, ny = y_ref.shape[1], a_ref.shape[1]
     a2[0:ny], a2[ny : 2 * ny] = a_ref[0], a_ref[0]
     step = 4
     for r in range(0, nx, step):
         res = dot(xhl[r * g : (r + step) * g, 0 : 2 * ny], a2[...])
-        y_ref[r : r + step] = res.reshape(step, g, res.shape[1])
+        y_ref[r : r + step] = res[:, 0 : y_ref.shape[2]].reshape(step, g, y_ref.shape[2])
+    lift = Lift(nx, lambda i: y_ref[i, :, 0:ny], edge_ref)
+    zero = jnp.zeros((g, TILE), F32)
+    top, begin, then = lift.detail(1, (nx >> 1) - 1), lift.detail(1, -1), lift.detail(1, 0)
+    row = lift.smooth(1, 0)
+    up = [top[:, 0:TILE], top[:, TILE:], zero, zero, zero]
+    down = [begin[:, 0:TILE], begin[:, TILE:], then[:, 0:TILE], then[:, TILE:], row[:, TILE:]]
+    to_pairs(var_ref[2], up, down, one_ref, two_ref)
+
+
+def to_pairs(odd, up, down, one_ref, two_ref):
+    for t, (a, b) in enumerate(zip(up, down)):
+        one_ref[t] = jnp.where(odd == 1, b, a)
+        two_ref[t] = jnp.where(odd == 1, a, b)
+
+
+def from_pairs(odd, one_ref, two_ref):
+    count = one_ref.shape[0]
+    below = [jnp.where(odd == 1, one_ref[t], two_ref[t]) for t in range(count)]
+    above = [jnp.where(odd == 1, two_ref[t], one_ref[t]) for t in range(count)]
+    return below, above
 
 
 class Lift:
@@ -280,10 +304,10 @@
 
 
 def send_kernel(nx, far, edge_ref, var_ref, yc_ref, ym_ref, one_ref, two_ref, p_ref, *rest):
-    up_ref, down_ref, cc_ref, z = rest[:4]
-    rest = rest[4:]
+    to_one_ref, to_two_ref, cc_ref, z, y2_ref = rest[:5]
+    rest = rest[5:]
     if far:
-        up2_ref, down2_ref = rest[:2]
+        far_one_ref, far_two_ref = rest[:2]
         rest = rest[2:]
     yc, yl, yh, p2 = rest
     g = yc.shape[1]
@@ -309,31 +333,22 @@
                 z[rows, c * TILE : (c + 1) * TILE] = jnp.where(here, pieces[j], zero)
     step = 4
     for r in range(0, nx, step):
-        res = dot(z[r * g : (r + step) * g], p2[:, mains : mains + TILE])
-        yc[r : r + step] = yc_ref[r : r + step] + res.reshape(step, g, TILE)
+        res = dot(z[r * g : (r + step) * g], p2[:, ny : mains + TILE])
+        y2_ref[r : r + step] = ym_ref[r : r + step, :, ny:mains] + res[:, 0:TILE].reshape(step, g, TILE)
+        yc[r : r + step] = yc_ref[r : r + step] + res[:, TILE:].reshape(step, g, TILE)
     low, high = yl.shape[0], yh.shape[0]
-    yl[...] = ym_ref[0:low] + dot(z[0 : low * g], p2[:, 0:mains]).reshape(yl.shape)
-    yh[...] = ym_ref[nx - high :] + dot(z[(nx - high) * g :], p2[:, 0:mains]).reshape(yh.shape)
-
-    def place(ref, tile, value):
-        for t in range(value.shape[1] // TILE):
-            ref[tile + t] = value[:, t * TILE : (t + 1) * TILE]
-
-    m1, m1d, m2 = slice(0, ny), slice(half, ny), slice(ny, ny + half)
-
-    def lift(ref, base, columns, first, last):
-        return Lift(nx, lambda i: ref[i - base, :, columns], edge_ref, first, last)
-
-    top = nx - high
-    place(up_ref, 0, lift(yh, top, m1, top, nx - 1).detail(1, n1 - 1))
-    one = lift(yh, top, m2, top, nx - 1)
-    up_ref[2], up_ref[3], up_ref[4] = one.detail(2, n2 - 1), one.detail(2, n2), one.smooth(2, n2)
-    one = lift(yl, 0, m1, 0, low - 1)
-    place(down_ref, 0, one.detail(1, -1))
-    place(down_ref, 2, one.detail(1, 0))
-    down_ref[4] = lift(yl, 0, m1d, 0, low - 1).smooth(1, 0)
-    one = lift(yl, 0, m2, 0, low - 1)
-    down_ref[5], down_ref[6], down_ref[7] = one.detail(2, -1), one.detail(2, 0), one.smooth(2, 0)
+    yl[...] = dot(z[0 : low * g], p2[:, 0:TILE]).reshape(yl.shape)
+    yh[...] = dot(z[(nx - high) * g :], p2[:, 0:TILE]).reshape(yh.shape)
+
+    def lift(ref, base):
+        return Lift(nx, lambda i: ref[i - base], edge_ref, base, base + ref.shape[0] - 1)
+
+    second = Lift(nx, lambda i: y2_ref[i], edge_ref)
+    one, two = lift(yl, 0), lift(yh, nx - high)
+    fix_up = [two.detail(1, n1 - 1)]
+    fix_down = [one.detail(1, -1), one.detail(1, 0), one.smooth(1, 0)]
+    up = [second.detail(2, n2 - 1), second.detail(2, n2), put_fixes(second.smooth(2, n2), fix_up)]
+    down = [second.detail(2, -1), second.detail(2, 0), put_fixes(second.smooth(2, 0), fix_down)]
 
     s_lanes = smooth_lanes(spans)
     deep = Lift(nx, lambda i: yc[i], edge_ref)
@@ -346,13 +361,26 @@
         n, here = nx >> k, in_span(spans[k])
         new = [deep.detail(k, n - 1)] + ([deep.detail(k, n), deep.smooth(k, n)] if k > 1 else [None] * 2)
         acc = [a if v is None else jnp.where(here, v, a) for a, v in zip(acc, new)]
-    for t in range(3):
-        up_ref[5 + t] = acc[t]
-    down_ref[8], down_ref[9], down_ref[10] = cc_ref[0], cc_ref[1], cc_ref[n1 + 1]
+    to_pairs(var_ref[2], up + acc, down + [cc_ref[0], cc_ref[1], cc_ref[n1 + 1]], to_one_ref, to_two_ref)
     if far:
         here = in_span(spans[LEVELS])
-        up2_ref[...] = jnp.where(here, deep.detail(LEVELS, nx >> LEVELS), 0.0)
-        down2_ref[...] = jnp.where(here, deep.detail(LEVELS, -1), 0.0)
+        up = jnp.where(here, deep.detail(LEVELS, nx >> LEVELS), 0.0)
+        down = jnp.where(here, deep.detail(LEVELS, -1), 0.0)
+        to_pairs(var_ref[3], [up], [down], far_one_ref, far_two_ref)
+
+
+def put_fixes(tile, fixes):
+    lane = lanes()
+    for j, fix in enumerate(fixes):
+        tile = jnp.where((lane >> 1) == j, pltpu.roll(fix, 1 + 2 * j, 1), tile)
+    return tile
+
+
+def get_fix(tile, j):
+    lane = lanes()
+    turned = pltpu.roll(tile, TILE - 1 - 2 * j, 1)
+    a = jnp.where((lane == 0) | (lane == TILE - 1), turned, 0.0)
+    return a, jnp.where(lane == TILE - 1, 4.0 * turned, 0.0)
 
 
 def weigh(r_ref, bands, value):
@@ -449,27 +477,27 @@
     return [(0, ny), c], [(half, ny), c]
 
 
-def local_kernel(nx, edge_ref, var_ref, ym_ref, z, cc_ref, p_ref, s_ref, r_ref,
+def local_kernel(nx, edge_ref, var_ref, ym_ref, z, y2_ref, cc_ref, p_ref, s_ref, r_ref,
                  vd_ref, vs_ref, w_ref, y, p2, zd, zs, sd, ss):
-    g, mains = y.shape[1], y.shape[2]
-    ny = mains - TILE
+    g, ny = y.shape[1], y.shape[2]
     _, spans = lane_plan(ny)
     n1, n2 = nx >> 1, nx >> 2
     plan, _ = weighted_plan(nx)
     n = 2 * TILE
-    p2[0:n], p2[n : 2 * n] = p_ref[:, 0:mains], p_ref[:, 0:mains]
+    p2[0:n], p2[n : 2 * n] = p_ref[:, 0:ny], p_ref[:, 0:ny]
     rows_d, rows_s = first_level_rows(ny)
     stack_back(s_ref, sd, rows_d)
     stack_back(s_ref, ss, rows_s)
     step = 4
     for r in range(0, nx, step):
         res = dot(z[r * g : (r + step) * g], p2[...])
-        y[r : r + step] = ym_ref[r : r + step] + res.reshape(step, g, mains)
+        y[r : r + step] = ym_ref[r : r + step, :, 0:ny] + res.reshape(step, g, ny)
 
     def lift(columns):
         return Lift(nx, lambda i: y[i, :, columns], edge_ref)
 
-    a, b, m2 = (lift(slice(t * TILE, (t + 1) * TILE)) for t in range(3))
+    a, b = (lift(slice(t * TILE, (t + 1) * TILE)) for t in range(2))
+    m2 = Lift(nx, lambda i: y2_ref[i], edge_ref)
 
     def store(name, low, some, tiles):
         for i, tile in zip(some, tiles):
@@ -512,12 +540,12 @@
         store(("m2", "s"), 0, some, weigh_m2(r_ref, "s", [m2.smooth(2, i) for i in some]))
 
 
-def final_kernel(nx, far, edge_ref, var_ref, vd_ref, vs_ref, w_ref, up_ref, down_ref, *rest):
+def final_kernel(nx, far, edge_ref, var_ref, vd_ref, vs_ref, w_ref, e_one, e_two, r_one, r_two, *rest):
     if far:
-        up2_ref, down2_ref = rest[:2]
+        f_one, f_two = rest[:2]
         rest = rest[2:]
     s_ref, r_ref, out_ref, sd, ss, sdeep, zd, zs, zdeep, rows, ot, sem = rest
-    g, ny = ot.shape[1], ot.shape[2]
+    g, ny = ot.shape[1], ot.shape[3]
     _, spans = lane_plan(ny)
     plan, _ = weighted_plan(nx)
     half = ny // 2
@@ -532,18 +560,25 @@
     def smooth_c(value):
         return jnp.where(s_lanes, 0.25 * value, 0.0)
 
-    c_d = {-1: up_ref[5], 0: up_ref[6], "n-1": down_ref[8], "n": down_ref[9]}
+    below, above = from_pairs(var_ref[2], r_one, r_two)
+    first_below, first_above = from_pairs(var_ref[2], e_one, e_two)
+    c_d = {-1: below[3], 0: below[4], "n-1": above[3], "n": above[4]}
     c_s = {
-        0: up_ref[7] + jnp.where(lev1, smooth_c(c_d[-1]), 0.0),
+        0: below[5] + jnp.where(lev1, smooth_c(c_d[-1]), 0.0),
         1: smooth_c(c_d[0]),
         "n-1": smooth_c(c_d["n-1"]),
-        "n": down_ref[10],
+        "n": above[5],
     }
     if far:
-        c_d[-1] = c_d[-1] + up2_ref[...]
-        c_s[0] = c_s[0] + smooth_c(up2_ref[...])
-        c_d["n"] = c_d["n"] + down2_ref[...]
-        c_s["n"] = c_s["n"] + smooth_c(down2_ref[...])
+        (far_below,), (far_above,) = from_pairs(var_ref[3], f_one, f_two)
+        c_d[-1] = c_d[-1] + far_below
+        c_s[0] = c_s[0] + smooth_c(far_below)
+        c_d["n"] = c_d["n"] + far_above
+        c_s["n"] = c_s["n"] + smooth_c(far_above)
+    fixes = [get_fix(below[2], 0)] + [get_fix(above[2], j) for j in range(3)]
+    a_tiles = [first_below[0] + fixes[0][0], first_above[0] + fixes[1][0], first_above[2] + fixes[2][0]]
+    b_tiles = [first_below[1] + fixes[0][1], first_above[1] + fixes[1][1], first_above[3] + fixes[2][1]]
+    s_tiles = [0.25 * b_tiles[0], 0.25 * b_tiles[1], first_above[4] + fixes[3][1]]
     every = list(range(1, LEVELS + 1))
     got = {}
 
@@ -554,18 +589,18 @@
     for kind, tiles in (("d", c_d), ("s", c_s)):
         keep(("c", kind), list(tiles), weigh_c(r_ref, spans, kind, every, list(tiles.values())))
     keys = [-1, "n-1", "n"]
-    ta = weigh_tiles(r_ref, band_of(1, "d", "s"), [up_ref[0], down_ref[0], down_ref[2]])
-    tb = weigh_tiles(r_ref, band_of(1, "d", "d"), [up_ref[1], down_ref[1], down_ref[3]])
+    ta = weigh_tiles(r_ref, band_of(1, "d", "s"), a_tiles)
+    tb = weigh_tiles(r_ref, band_of(1, "d", "d"), b_tiles)
     for j, key in enumerate(keys):
         pairs_into(zd, j, g, [ta[j], tb[j], jnp.where(lev1, got[("c", "d"), key], 0.0)])
     more_d = dot(zd[...], sd[...])
-    tb = weigh_tiles(r_ref, band_of(1, "s", "d"), [0.25 * up_ref[1], 0.25 * down_ref[1], down_ref[4]])
+    tb = weigh_tiles(r_ref, band_of(1, "s", "d"), s_tiles)
     for j, key in enumerate([0, "n-1", "n"]):
         pairs_into(zs, j, g, [tb[j], jnp.where(lev1, got[("c", "s"), key], 0.0)])
     more_s = dot(zs[...], ss[...])
-    keep(("m2", "d"), [-1, 0, "n-1", "n"], weigh_m2(r_ref, "d", [up_ref[2], up_ref[3], down_ref[5], down_ref[6]]))
+    keep(("m2", "d"), [-1, 0, "n-1", "n"], weigh_m2(r_ref, "d", [below[0], below[1], above[0], above[1]]))
     keep(("m2", "s"), [0, 1, "n-1", "n"],
-         weigh_m2(r_ref, "s", [up_ref[4], 0.25 * up_ref[3], 0.25 * down_ref[5], down_ref[7]]))
+         weigh_m2(r_ref, "s", [below[2], 0.25 * below[1], 0.25 * above[0], above[2]]))
 
     def value_of(array, kind, k, i):
         n, low = nx >> k, -1 if kind == "d" else 0
@@ -634,10 +669,17 @@
 
     copies = []
 
+    pending = {}
+
     def emit_out(i, value):
-        if i < nx:
-            ot[i] = value
-            copies.append(pltpu.make_async_copy(ot.at[i], out_ref.at[:, i], sem.at[i]))
+        if i >= nx:
+            return
+        pending[i] = value
+        r = i - i % 8
+        if all(j in pending for j in range(r, r + 8)):
+            block = jnp.stack([pending.pop(j) for j in range(r, r + 8)], 0)
+            ot[r // 8] = jnp.swapaxes(block, 0, 1)
+            copies.append(pltpu.make_async_copy(ot.at[r // 8], out_ref.at[:, pl.ds(r, 8)], sem.at[r // 8]))
             copies[-1].start()
 
     unlift(n1, smooth_first, detail_first, emit_out)
@@ -649,16 +691,10 @@
     return sum((nx >> j) + 1 for j in range(max(k + 1, 3), LEVELS)) if k > 1 else 0
 
 
-def shift(value, axis, step):
+def swap(value, axis, first, step=1):
     count = lax.axis_size(axis)
-    pairs = [(i, i + step) for i in range(count) if 0 <= i + step < count]
-    return lax.ppermute(value, axis, pairs)
-
-
-def swap(value, axis, first):
-    count = lax.axis_size(axis)
-    starts = range(first, count - 1, 2)
-    return lax.ppermute(value, axis, [p for i in starts for p in ((i, i + 1), (i + 1, i))])
+    starts = [i for i in range(first, count - step) if (i - first) // step % 2 == 0]
+    return lax.ppermute(value, axis, [p for i in starts for p in ((i, i + step), (i + step, i))])
 
 
 def per_device(control, band_roots):
@@ -677,7 +713,7 @@
     ix, iy = lax.axis_index("gx"), lax.axis_index("gy")
     edge = jnp.stack([ix > 0, ix < gx - 1]).astype(F32)
     which = jnp.where(iy == 0, 0, jnp.where(iy == gy - 1, 2, 1)) if gy > 1 else jnp.zeros((), jnp.int32)
-    which = jnp.stack([which, iy % 2, ix % 2]).astype(jnp.int32)
+    which = jnp.stack([which, iy % 2, ix % 2, ix // 2 % 2]).astype(jnp.int32)
     r_hi = lax.reduce_precision(band_roots, 8, 7)
     r_lo = band_roots - r_hi
     roots = jnp.concatenate([r_hi.astype(BF), r_lo.astype(BF), r_hi.astype(BF)], 2)
@@ -711,44 +747,45 @@
         partial(first_kernel, nx),
         [(pltpu.with_memory_space_constraint(t, pltpu.HBM), far_hbm) for t in (rows3, ehi_mat, elo_mat)],
         [((nx * g, 3 * ny), BF), ((nx,) + tile, F32), ((nx // per,) + tile, F32), ((nx // per,) + tile, F32)],
-        [pltpu.VMEM((nx, g, ny), F32), pltpu.VMEM((3 * ny, 2 * TILE), BF), pltpu.SemaphoreType.DMA((nx + 3,))],
+        [pltpu.VMEM((nx // per, g, per, ny), F32), pltpu.VMEM((3 * ny, 2 * TILE), BF), pltpu.SemaphoreType.DMA((nx + 3,))],
         "first",
     )
     got_one = swap(one, "gy", 0)
     got_two = swap(two, "gy", 1)
-    (ym,) = call(
+    ym, one, two = call(
         partial(main_kernel, nx),
         [(xhl, vmem), variant(main_mat)],
-        [((nx, g, mains), F32)],
-        [pltpu.VMEM((2 * ny, mains), BF)],
+        [((nx, g, mains), F32), ((5,) + tile, F32), ((5,) + tile, F32)],
+        [pltpu.VMEM((2 * ny, mains + TILE), BF)],
         "main",
     )
+    got = [(swap(one, "gx", 0), vmem), (swap(two, "gx", 1), vmem)]
     slots = 2 * n1 + 2
     sent = call(
         partial(send_kernel, nx, far),
         [(yc, vmem), (ym, vmem), (got_one, vmem), (got_two, vmem), (p_mat, vmem)],
-        [((8,) + tile, F32), ((11,) + tile, F32), ((slots,) + tile, F32), ((nx * g, 4 * TILE), BF)]
-        + ([(tile, F32), (tile, F32)] if far else []),
+        [((6,) + tile, F32), ((6,) + tile, F32), ((slots,) + tile, F32), ((nx * g, 4 * TILE), BF), ((nx,) + tile, F32)]
+        + ([((1,) + tile, F32)] * 2 if far else []),
         [
             pltpu.VMEM((nx,) + tile, F32),
-            pltpu.VMEM((8, g, mains), F32),
-            pltpu.VMEM((8, g, mains), F32),
+            pltpu.VMEM((4,) + tile, F32),
+            pltpu.VMEM((4,) + tile, F32),
             pltpu.VMEM((4 * TILE, mains + TILE), BF),
         ],
         "send",
     )
-    got = [(shift(sent[0], "gx", 1), vmem), (shift(sent[1], "gx", -1), vmem)]
+    got += [(swap(sent[0], "gx", 0), vmem), (swap(sent[1], "gx", 1), vmem)]
     if far:
-        got += [(shift(sent[4], "gx", 2), vmem), (shift(sent[5], "gx", -2), vmem)]
+        got += [(swap(sent[5], "gx", 0, 2), vmem), (swap(sent[6], "gx", 2, 2), vmem)]
 
     _, count = weighted_plan(nx)
     vd, vs, w = call(
         partial(local_kernel, nx),
-        [(ym, vmem), (sent[3], vmem), (sent[2], vmem), (p_mat, vmem), variant(s_mat), (roots, vmem)],
+        [(ym, vmem), (sent[3], vmem), (sent[4], vmem), (sent[2], vmem), (p_mat, vmem), variant(s_mat), (roots, vmem)],
         [((n1 + 1, g, ny), F32), ((n1 + 1, g, ny), F32), ((count,) + tile, F32)],
         [
-            pltpu.VMEM((nx, g, mains), F32),
-            pltpu.VMEM((4 * TILE, mains), BF),
+            pltpu.VMEM((nx, g, ny), F32),
+            pltpu.VMEM((4 * TILE, ny), BF),
             pltpu.VMEM(((n1 + 1) * g, 6 * TILE), BF),
             pltpu.VMEM(((n1 + 1) * g, 4 * TILE), BF),
             pltpu.VMEM((6 * TILE, ny), BF),
@@ -768,8 +805,8 @@
             pltpu.VMEM((3 * g, 4 * TILE), BF),
             pltpu.VMEM(((n1 + 1) * g, 4 * TILE), BF),
             pltpu.VMEM((level_base(nx, 1) + sum((nx >> j) + 1 for j in range(2, LEVELS)),) + tile, F32),
-            pltpu.VMEM((nx, g, ny), F32),
-            pltpu.SemaphoreType.DMA((nx,)),
+            pltpu.VMEM((nx // 8, g, 8, ny), F32),
+            pltpu.SemaphoreType.DMA((nx // 8,)),
         ],
         "final",
         (hbm,),

time: 35.3 us -> 31.3 us (0.89)
  the two profiles are of different devices: /device:TPU:19 before, /device:TPU:12 now
where the time goes in v1:
time: 31.3 us; the launch traced here: 31.1 us
  starting transfers between devices  15.9 us (51%)
  Pallas kernels  14.6 us (47%)
  other arithmetic  0.34 us (1%)
    ppermute x8, starting transfers between devices, swap(): lax.ppermute(value, axis, [p for i in starts for p in ((i, i + step), (i...  15.9 us
    pallas_call x5, Pallas kernels, call(): pl.pallas_call(kernel, out_shape=tuple((jax.ShapeDtypeStruct(*s) for s in...  14.6 us
  transfers between devices with their start and end apart: 8, of which 0 were waited for; matrix products, arithmetic and copies ran while one was open for 1% of the time, Pallas kernels for 17%

profile of v1, /device:TPU:12, one launch (start us, length us, event | category | flops | bytes accessed | tf_op | source)
XLA Modules:
  0.0 31.1 jit_solution(10063054345731854677)
XLA Ops:
  0.0 0.0 copy-start.2
  0.0 0.1 add_convert_fusion.edge_ref
  0.1 0.1 pad_add_fusion.var_ref
  0.2 4.1 %first.1 = (bf16[2048,768]{1,0:T(8,128)(2,1)S(1)}, f32[32,64,128]{2,1,0:T(8,128)S(1)}, f32[4,64,128]{2,1,0:T(8,128)S(1)}, f32[4,64,128]{2,1,0:T(8,128)S(1)}) custom-call(f32[2]{0:T(128)S(1)} %add_convert_fusion.edge_ref, s32[4]{0:T(128)S(1)} %pad_add_fusion.var_ref, f32[64,32,256]{2,1,0:T(8,128)} %bitcast.8, bf16[3,256,256]{2,1,0:T(8,128)(2,1)} %constant.58.clone.ehi_ref, ...), custom_call_target="tpu_custom_call" | custom-call | tf_op jit(solution)/shard_map/first/pallas_call | solution.py:729
  4.3 0.0 copy-start.1
  4.3 0.1 collective-permute-start
  4.4 2.4 %collective-permute-start.1 = (f32[4,64,128]{2,1,0:T(8,128)S(1)}, f32[4,64,128]{2,1,0:T(8,128)S(1)}, u32[]{:S(2)}, u32[]{:S(2)}) collective-permute-start(f32[4,64,128]{2,1,0:T(8,128)S(1)} %get-tuple-element.26), channel_id=1, source_target_pairs={{1,2},{2,1},{5,6},{6,5},{9,10},{10,9},{13,14},{14,13},{17,18},{18,... | collective-permute-start | bytes 393224 | tf_op jit(solution)/shard_map/ppermute | solution.py:697
  6.8 0.0 copy-done.2
  6.8 1.8 %main.1 = (f32[32,64,384]{2,1,0:T(8,128)S(1)}, f32[5,64,128]{2,1,0:T(8,128)S(1)}, f32[5,64,128]{2,1,0:T(8,128)S(1)}) custom-call(f32[2]{0:T(128)S(1)} %add_convert_fusion.edge_ref, s32[4]{0:T(128)S(1)} %pad_add_fusion.var_ref, bf16[2048,768]{1,0:T(8,128)(2,1)S(1)} %get-tuple-element.22.xhl, bf16[3,256,512]{2,1,0:T(8,128)(2,1)S(1)} %copy-done.2), custom_call_target="tpu_custom_call" | custom-call | tf_op jit(solution)/shard_map/main/pallas_call | solution.py:729
  8.6 1.6 %collective-permute-start.2 = (f32[5,64,128]{2,1,0:T(8,128)S(1)}, f32[5,64,128]{2,1,0:T(8,128)S(1)}, u32[]{:S(2)}, u32[]{:S(2)}) collective-permute-start(f32[5,64,128]{2,1,0:T(8,128)S(1)} %get-tuple-element.33), channel_id=1, source_target_pairs={{0,4},{4,0},{8,12},{12,8},{16,20},{20,16},{24,28},{28,24},{1,5},{5... | collective-permute-start | bytes 491528 | tf_op jit(solution)/shard_map/ppermute | solution.py:697
  10.2 1.9 %collective-permute-start.3 = (f32[5,64,128]{2,1,0:T(8,128)S(1)}, f32[5,64,128]{2,1,0:T(8,128)S(1)}, u32[]{:S(2)}, u32[]{:S(2)}) collective-permute-start(f32[5,64,128]{2,1,0:T(8,128)S(1)} %get-tuple-element.34), channel_id=1, source_target_pairs={{4,8},{8,4},{12,16},{16,12},{20,24},{24,20},{5,9},{9,5},{13,17},{1... | collective-permute-start | bytes 491528 | tf_op jit(solution)/shard_map/ppermute | solution.py:697
  12.1 0.0 collective-permute-done.one_ref
  12.1 0.0 collective-permute-done.1.two_ref
  12.1 0.0 copy-done.1
  12.1 0.0 copy-start.3
  12.1 0.0 copy-start
  12.1 1.8 %send.1 = (f32[6,64,128]{2,1,0:T(8,128)S(1)}, f32[6,64,128]{2,1,0:T(8,128)S(1)}, f32[34,64,128]{2,1,0:T(8,128)S(1)}, bf16[2048,512]{1,0:T(8,128)(2,1)S(1)}, f32[...) custom-call(f32[2]{0:T(128)S(1)} %add_convert_fusion.edge_ref, ...), custom_call_target="tpu_custom_call" | custom-call | tf_op jit(solution)/shard_map/send/pallas_call | solution.py:729
  14.0 3.1 %collective-permute-start.4 = (f32[6,64,128]{2,1,0:T(8,128)S(1)}, f32[6,64,128]{2,1,0:T(8,128)S(1)}, u32[]{:S(2)}, u32[]{:S(2)}) collective-permute-start(f32[6,64,128]{2,1,0:T(8,128)S(1)} %get-tuple-element.35), channel_id=1, source_target_pairs={{0,4},{4,0},{8,12},{12,8},{16,20},{20,16},{24,28},{28,24},{1,5},{5... | collective-permute-start | bytes 589832 | tf_op jit(solution)/shard_map/ppermute | solution.py:697
  17.0 1.9 %collective-permute-start.5 = (f32[6,64,128]{2,1,0:T(8,128)S(1)}, f32[6,64,128]{2,1,0:T(8,128)S(1)}, u32[]{:S(2)}, u32[]{:S(2)}) collective-permute-start(f32[6,64,128]{2,1,0:T(8,128)S(1)} %get-tuple-element.36), channel_id=1, source_target_pairs={{4,8},{8,4},{12,16},{16,12},{20,24},{24,20},{5,9},{9,5},{13,17},{1... | collective-permute-start | bytes 589832 | tf_op jit(solution)/shard_map/ppermute | solution.py:697
  19.0 0.0 copy-done.3
  19.0 0.1 collective-permute-start.6
  19.1 0.0 collective-permute-done.2.e_one
  19.1 4.9 %collective-permute-start.7 = (f32[1,64,128]{2,1,0:T(8,128)S(1)}, f32[1,64,128]{2,1,0:T(8,128)S(1)}, u32[]{:S(2)}, u32[]{:S(2)}) collective-permute-start(f32[1,64,128]{2,1,0:T(8,128)S(1)} %get-tuple-element.38), channel_id=1, source_target_pairs={{8,16},{16,8},{12,20},{20,12},{9,17},{17,9},{13,21},{21,13},{10,18... | collective-permute-start | bytes 98312 | tf_op jit(solution)/shard_map/ppermute | solution.py:697
  24.1 0.1 pad_maximum_fusion.r_ref.rest_3_
  24.2 0.0 copy-done
  24.2 3.5 %local.1 = (f32[17,64,256]{2,1,0:T(8,128)S(1)}, f32[17,64,256]{2,1,0:T(8,128)S(1)}, f32[38,64,128]{2,1,0:T(8,128)S(1)}) custom-call(f32[2]{0:T(128)S(1)} %add_convert_fusion.edge_ref, s32[4]{0:T(128)S(1)} %pad_add_fusion.var_ref, f32[32,64,384]{2,1,0:T(8,128)S(1)} %get-tuple-element.23.ym_ref, bf16[2048,512]{1,0:T(8,128)(2,1)S(1)} %get-tuple-element.27.z, ...), custom_call_target="tpu_custom_call" | custom-call | tf_op jit(solution)/shard_map/local/pallas_call | solution.py:729
  27.7 0.0 collective-permute-done.3.e_two
  27.7 0.0 collective-permute-done.6.rest_0_
  27.7 0.0 collective-permute-done.7.rest_1_
  27.7 0.0 collective-permute-done.4.r_one
  27.7 0.0 collective-permute-done.5.r_two
  27.7 3.4 %final.1 = f32[64,32,256]{2,1,0:T(8,128)} custom-call(f32[2]{0:T(128)S(1)} %add_convert_fusion.edge_ref, s32[4]{0:T(128)S(1)} %pad_add_fusion.var_ref, f32[17,64,256]{2,1,0:T(8,128)S(1)} %get-tuple-element.30.vd_ref, f32[17,64,256]{2,1,0:T(8,128)S(1)} %get-tuple-element.31.vs_ref, f32[38,64,128]{2,1,0:T(8,128)S(1)} %get-tuple-element.32.w_ref, ...), custom_call_target="tpu_custom_call" | custom-call | tf_op jit(solution)/shard_map/final/pallas_call | solution.py:729
  (1 shorter events, 0.0 us)
Async XLA Ops:
  0.0 6.8 %copy-start.2 = (bf16[3,256,512]{2,1,0:T(8,128)(2,1)S(1)}, bf16[3,256,512]{2,1,0:T(8,128)(2,1)}, u32[]{:S(2)}) copy-start(bf16[3,256,512]{2,1,0:T(8,128)(2,1)} %constant.57.clone.a_ref) | copy-start | bytes 2359300
  4.3 7.8 %copy-start.1 = (bf16[256,512]{1,0:T(8,128)(2,1)S(1)}, bf16[256,512]{1,0:T(8,128)(2,1)}, u32[]{:S(2)}) copy-start(bf16[256,512]{1,0:T(8,128)(2,1)} %constant.61.clone.p_ref) | copy-start | bytes 786436
  4.3 7.8 %collective-permute-start = (f32[4,64,128]{2,1,0:T(8,128)S(1)}, f32[4,64,128]{2,1,0:T(8,128)S(1)}, u32[]{:S(2)}, u32[]{:S(2)}) collective-permute-start(f32[4,64,128]{2,1,0:T(8,128)S(1)} %get-tuple-element.25), channel_id=1, source_target_pairs={{0,1},{1,0},{2,3},{3,2},{4,5},{5,4},{6,7},{7,6},{8,9},{9,8},{10,11... | collective-permute-start | bytes 393224 | tf_op jit(solution)/shard_map/ppermute | solution.py:697
  4.4 7.7 %collective-permute-start.1 = (f32[4,64,128]{2,1,0:T(8,128)S(1)}, f32[4,64,128]{2,1,0:T(8,128)S(1)}, u32[]{:S(2)}, u32[]{:S(2)}) collective-permute-start(f32[4,64,128]{2,1,0:T(8,128)S(1)} %get-tuple-element.26), channel_id=1, source_target_pairs={{1,2},{2,1},{5,6},{6,5},{9,10},{10,9},{13,14},{14,13},{17,18},{18,... | collective-permute-start | bytes 393224 | tf_op jit(solution)/shard_map/ppermute | solution.py:697
  8.6 10.5 %collective-permute-start.2 = (f32[5,64,128]{2,1,0:T(8,128)S(1)}, f32[5,64,128]{2,1,0:T(8,128)S(1)}, u32[]{:S(2)}, u32[]{:S(2)}) collective-permute-start(f32[5,64,128]{2,1,0:T(8,128)S(1)} %get-tuple-element.33), channel_id=1, source_target_pairs={{0,4},{4,0},{8,12},{12,8},{16,20},{20,16},{24,28},{28,24},{1,5},{5... | collective-permute-start | bytes 491528 | tf_op jit(solution)/shard_map/ppermute | solution.py:697
  10.2 17.5 %collective-permute-start.3 = (f32[5,64,128]{2,1,0:T(8,128)S(1)}, f32[5,64,128]{2,1,0:T(8,128)S(1)}, u32[]{:S(2)}, u32[]{:S(2)}) collective-permute-start(f32[5,64,128]{2,1,0:T(8,128)S(1)} %get-tuple-element.34), channel_id=1, source_target_pairs={{4,8},{8,4},{12,16},{16,12},{20,24},{24,20},{5,9},{9,5},{13,17},{1... | collective-permute-start | bytes 491528 | tf_op jit(solution)/shard_map/ppermute | solution.py:697
  12.1 6.8 %copy-start.3 = (f32[16,32,32]{2,1,0:T(8,128)S(1)}, f32[16,32,32]{2,1,0:T(8,128)}, u32[]{:S(2)}) copy-start(f32[16,32,32]{2,1,0:T(8,128)} %param.8) | copy-start | bytes 196612
  12.1 12.1 %copy-start = (bf16[3,512,256]{2,1,0:T(8,128)(2,1)S(1)}, bf16[3,512,256]{2,1,0:T(8,128)(2,1)}, u32[]{:S(2)}) copy-start(bf16[3,512,256]{2,1,0:T(8,128)(2,1)} %constant.60.clone.s_ref.rest_2_) | copy-start | bytes 2359300
  14.0 13.7 %collective-permute-start.4 = (f32[6,64,128]{2,1,0:T(8,128)S(1)}, f32[6,64,128]{2,1,0:T(8,128)S(1)}, u32[]{:S(2)}, u32[]{:S(2)}) collective-permute-start(f32[6,64,128]{2,1,0:T(8,128)S(1)} %get-tuple-element.35), channel_id=1, source_target_pairs={{0,4},{4,0},{8,12},{12,8},{16,20},{20,16},{24,28},{28,24},{1,5},{5... | collective-permute-start | bytes 589832 | tf_op jit(solution)/shard_map/ppermute | solution.py:697
  17.0 10.7 %collective-permute-start.5 = (f32[6,64,128]{2,1,0:T(8,128)S(1)}, f32[6,64,128]{2,1,0:T(8,128)S(1)}, u32[]{:S(2)}, u32[]{:S(2)}) collective-permute-start(f32[6,64,128]{2,1,0:T(8,128)S(1)} %get-tuple-element.36), channel_id=1, source_target_pairs={{4,8},{8,4},{12,16},{16,12},{20,24},{24,20},{5,9},{9,5},{13,17},{1... | collective-permute-start | bytes 589832 | tf_op jit(solution)/shard_map/ppermute | solution.py:697
  19.0 8.7 %collective-permute-start.6 = (f32[1,64,128]{2,1,0:T(8,128)S(1)}, f32[1,64,128]{2,1,0:T(8,128)S(1)}, u32[]{:S(2)}, u32[]{:S(2)}) collective-permute-start(f32[1,64,128]{2,1,0:T(8,128)S(1)} %get-tuple-element.37), channel_id=1, source_target_pairs={{0,8},{8,0},{4,12},{12,4},{16,24},{24,16},{20,28},{28,20},{1,9},{9... | collective-permute-start | bytes 98312 | tf_op jit(solution)/shard_map/ppermute | solution.py:697
  19.1 8.6 %collective-permute-start.7 = (f32[1,64,128]{2,1,0:T(8,128)S(1)}, f32[1,64,128]{2,1,0:T(8,128)S(1)}, u32[]{:S(2)}, u32[]{:S(2)}) collective-permute-start(f32[1,64,128]{2,1,0:T(8,128)S(1)} %get-tuple-element.38), channel_id=1, source_target_pairs={{8,16},{16,8},{12,20},{20,12},{9,17},{17,9},{13,21},{21,13},{10,18... | collective-permute-start | bytes 98312 | tf_op jit(solution)/shard_map/ppermute | solution.py:697

commit v2 on v1

--- a/solution.py
+++ b/solution.py
@@ -164,6 +164,13 @@
 def in_span(span):
     lane = lanes()
     return (lane >= span[0]) & (lane < span[1])
+
+
+def device_place(gx, gy):
+    ix, iy = lax.axis_index("gx"), lax.axis_index("gy")
+    edge = jnp.where(ix > 0, 1.0, 0.0), jnp.where(ix < gx - 1, 1.0, 0.0)
+    kind = jnp.where(iy == 0, 0, jnp.where(iy == gy - 1, 2, 1)) if gy > 1 else 0
+    return edge, (kind, lax.rem(iy, 2), lax.rem(ix, 2), lax.rem(ix // 2, 2))
 
 
 def first_kernel(nx, edge_ref, var_ref, x_ref, ehi_ref, elo_ref, xhl, yc_ref, one_ref, two_ref, xt, e3, sems):
@@ -208,7 +215,7 @@
 
 def main_kernel(nx, edge_ref, var_ref, xhl, a_ref, y_ref, one_ref, two_ref, a2):
     g, ny = y_ref.shape[1], a_ref.shape[1]
-    a2[0:ny], a2[ny : 2 * ny] = a_ref[0], a_ref[0]
+    a2[0:ny], a2[ny : 2 * ny] = a_ref[var_ref[0]], a_ref[var_ref[0]]
     step = 4
     for r in range(0, nx, step):
         res = dot(xhl[r * g : (r + step) * g, 0 : 2 * ny], a2[...])
@@ -465,10 +472,10 @@
         ref[rows, cols], ref[rows, width + t * TILE : width + (t + 1) * TILE] = split(tile)
 
 
-def stack_back(s_ref, out, spans_of_rows):
+def stack_back(s_ref, which, out, spans_of_rows):
     at = 0
     for a, b in spans_of_rows * 2:
-        out[at : at + b - a] = s_ref[0, a:b]
+        out[at : at + b - a] = s_ref[which, a:b]
         at += b - a
 
 
@@ -486,8 +493,8 @@
     n = 2 * TILE
     p2[0:n], p2[n : 2 * n] = p_ref[:, 0:ny], p_ref[:, 0:ny]
     rows_d, rows_s = first_level_rows(ny)
-    stack_back(s_ref, sd, rows_d)
-    stack_back(s_ref, ss, rows_s)
+    stack_back(s_ref, var_ref[0], sd, rows_d)
+    stack_back(s_ref, var_ref[0], ss, rows_s)
     step = 4
     for r in range(0, nx, step):
         res = dot(z[r * g : (r + step) * g], p2[...])
@@ -551,9 +558,9 @@
     half = ny // 2
     n1, n2 = nx >> 1, nx >> 2
     rows_d, rows_s = first_level_rows(ny)
-    stack_back(s_ref, sd, rows_d)
-    stack_back(s_ref, ss, rows_s)
-    stack_back(s_ref, sdeep, [(ny, ny + half + TILE)])
+    stack_back(s_ref, var_ref[0], sd, rows_d)
+    stack_back(s_ref, var_ref[0], ss, rows_s)
+    stack_back(s_ref, var_ref[0], sdeep, [(ny, ny + half + TILE)])
     s_lanes = smooth_lanes(spans)
     lev1 = in_span(spans[1])
 
@@ -710,10 +717,6 @@
     n1, n2 = nx >> 1, nx >> 2
     mains = ny + half
 
-    ix, iy = lax.axis_index("gx"), lax.axis_index("gy")
-    edge = jnp.stack([ix > 0, ix < gx - 1]).astype(F32)
-    which = jnp.where(iy == 0, 0, jnp.where(iy == gy - 1, 2, 1)) if gy > 1 else jnp.zeros((), jnp.int32)
-    which = jnp.stack([which, iy % 2, ix % 2, ix // 2 % 2]).astype(jnp.int32)
     r_hi = lax.reduce_precision(band_roots, 8, 7)
     r_lo = band_roots - r_hi
     roots = jnp.concatenate([r_hi.astype(BF), r_lo.astype(BF), r_hi.astype(BF)], 2)
@@ -721,24 +724,19 @@
     hbm = pl.BlockSpec(memory_space=pl.ANY)
     vmem = pl.BlockSpec(memory_space=pltpu.VMEM)
 
-    def variant(mat):
-        shape = (1,) + mat.shape[1:]
-        return mat, pl.BlockSpec(shape, lambda i, e, v: (v[0], 0, 0))
-
     def call(kernel, ins, outs, scratches, name, out_specs=None):
+        def body(*refs):
+            kernel(*device_place(gx, gy), *refs)
+
         return pl.pallas_call(
-            kernel,
+            body,
             out_shape=tuple(jax.ShapeDtypeStruct(*s) for s in outs),
-            grid_spec=pltpu.PrefetchScalarGridSpec(
-                num_scalar_prefetch=2,
-                grid=(1,),
-                in_specs=[s for _, s in ins],
-                out_specs=out_specs or (vmem,) * len(outs),
-                scratch_shapes=scratches,
-            ),
+            in_specs=[s for _, s in ins],
+            out_specs=out_specs or (vmem,) * len(outs),
+            scratch_shapes=scratches,
             name=name,
             compiler_params=pltpu.CompilerParams(vmem_limit_bytes=VMEM_LIMIT),
-        )(edge, which, *[a for a, _ in ins])
+        )(*[a for a, _ in ins])
 
     tile = (g, TILE)
     rows3 = control.reshape(g, nx, ny)
@@ -754,7 +752,7 @@
     got_two = swap(two, "gy", 1)
     ym, one, two = call(
         partial(main_kernel, nx),
-        [(xhl, vmem), variant(main_mat)],
+        [(xhl, vmem), (main_mat, vmem)],
         [((nx, g, mains), F32), ((5,) + tile, F32), ((5,) + tile, F32)],
         [pltpu.VMEM((2 * ny, mains + TILE), BF)],
         "main",
@@ -781,7 +779,7 @@
     _, count = weighted_plan(nx)
     vd, vs, w = call(
         partial(local_kernel, nx),
-        [(ym, vmem), (sent[3], vmem), (sent[4], vmem), (sent[2], vmem), (p_mat, vmem), variant(s_mat), (roots, vmem)],
+        [(ym, vmem), (sent[3], vmem), (sent[4], vmem), (sent[2], vmem), (p_mat, vmem), (s_mat, vmem), (roots, vmem)],
         [((n1 + 1, g, ny), F32), ((n1 + 1, g, ny), F32), ((count,) + tile, F32)],
         [
             pltpu.VMEM((nx, g, ny), F32),
@@ -795,7 +793,7 @@
     )
     (out,) = call(
         partial(final_kernel, nx, far),
-        [(vd, vmem), (vs, vmem), (w, vmem)] + got + [variant(s_mat), (roots, vmem)],
+        [(vd, vmem), (vs, vmem), (w, vmem)] + got + [(s_mat, vmem), (roots, vmem)],
         [((g, nx, ny), F32)],
         [
             pltpu.VMEM((6 * TILE, ny), BF),

time: 31.3 us -> 28.6 us (0.914)
  the two profiles are of different devices: /device:TPU:12 before, /device:TPU:17 now
where the time goes in v2:
time: 28.6 us; the launch traced here: 28.4 us
  starting transfers between devices  14.6 us (51%)
  Pallas kernels  11.7 us (41%)
  waiting for transfers between devices  1.75 us (6%)
    ppermute x8, starting transfers between devices, swap(): lax.ppermute(value, axis, [p for i in starts for p in ((i, i + step), (i...  14.6 us
    pallas_call x5, Pallas kernels, call(): pl.pallas_call(body, out_shape=tuple((jax.ShapeDtypeStruct(*s) for s in o...  11.7 us
    ppermute x8, waiting for transfers between devices, swap(): lax.ppermute(value, axis, [p for i in starts for p in ((i, i + step), (i...  1.75 us
  transfers between devices with their start and end apart: 8, of which 1 were waited for; matrix products, arithmetic and copies ran while one was open for 1% of the time, Pallas kernels for 14%

profile of v2, /device:TPU:17, one launch (start us, length us, event | category | flops | bytes accessed | tf_op | source)
XLA Modules:
  0.0 28.4 jit_solution(8570181031137580621)
XLA Ops:
  0.0 0.0 copy-start.2
  0.0 3.6 %first.1 = (bf16[2048,768]{1,0:T(8,128)(2,1)S(1)}, f32[32,64,128]{2,1,0:T(8,128)S(1)}, f32[4,64,128]{2,1,0:T(8,128)S(1)}, f32[4,64,128]{2,1,0:T(8,128)S(1)}) custom-call(f32[64,32,256]{2,1,0:T(8,128)} %bitcast.2, bf16[3,256,256]{2,1,0:T(8,128)(2,1)} %constant.11.clone.refs_1_, bf16[3,256,256]{2,1,0:T(8,128)(2,1)} %constant.12.clone.refs_2_), custom_call_target="tpu_custom_call" | custom-call | tf_op jit(solution)/shard_map/first/pallas_call | solution.py:731
  3.6 0.0 copy-start.1
  3.6 0.7 %collective-permute-start = (f32[4,64,128]{2,1,0:T(8,128)S(1)}, f32[4,64,128]{2,1,0:T(8,128)S(1)}, u32[]{:S(2)}, u32[]{:S(2)}) collective-permute-start(f32[4,64,128]{2,1,0:T(8,128)S(1)} %get-tuple-element.25), channel_id=1, source_target_pairs={{0,1},{1,0},{2,3},{3,2},{4,5},{5,4},{6,7},{7,6},{8,9},{9,8},{10,11... | collective-permute-start | bytes 393224 | tf_op jit(solution)/shard_map/ppermute | solution.py:704
  4.3 3.1 %collective-permute-start.1 = (f32[4,64,128]{2,1,0:T(8,128)S(1)}, f32[4,64,128]{2,1,0:T(8,128)S(1)}, u32[]{:S(2)}, u32[]{:S(2)}) collective-permute-start(f32[4,64,128]{2,1,0:T(8,128)S(1)} %get-tuple-element.26), channel_id=1, source_target_pairs={{1,2},{2,1},{5,6},{6,5},{9,10},{10,9},{13,14},{14,13},{17,18},{18,... | collective-permute-start | bytes 393224 | tf_op jit(solution)/shard_map/ppermute | solution.py:704
  7.4 0.0 copy-done.2
  7.4 1.3 %main.1 = (f32[32,64,384]{2,1,0:T(8,128)S(1)}, f32[5,64,128]{2,1,0:T(8,128)S(1)}, f32[5,64,128]{2,1,0:T(8,128)S(1)}) custom-call(bf16[2048,768]{1,0:T(8,128)(2,1)S(1)} %get-tuple-element.22.refs_0_, bf16[3,256,512]{2,1,0:T(8,128)(2,1)S(1)} %copy-done.2), custom_call_target="tpu_custom_call" | custom-call | tf_op jit(solution)/shard_map/main/pallas_call | solution.py:731
  8.7 1.3 %collective-permute-start.2 = (f32[5,64,128]{2,1,0:T(8,128)S(1)}, f32[5,64,128]{2,1,0:T(8,128)S(1)}, u32[]{:S(2)}, u32[]{:S(2)}) collective-permute-start(f32[5,64,128]{2,1,0:T(8,128)S(1)} %get-tuple-element.33), channel_id=1, source_target_pairs={{0,4},{4,0},{8,12},{12,8},{16,20},{20,16},{24,28},{28,24},{1,5},{5... | collective-permute-start | bytes 491528 | tf_op jit(solution)/shard_map/ppermute | solution.py:704
  10.0 2.0 %collective-permute-start.3 = (f32[5,64,128]{2,1,0:T(8,128)S(1)}, f32[5,64,128]{2,1,0:T(8,128)S(1)}, u32[]{:S(2)}, u32[]{:S(2)}) collective-permute-start(f32[5,64,128]{2,1,0:T(8,128)S(1)} %get-tuple-element.34), channel_id=1, source_target_pairs={{4,8},{8,4},{12,16},{16,12},{20,24},{24,20},{5,9},{9,5},{13,17},{1... | collective-permute-start | bytes 491528 | tf_op jit(solution)/shard_map/ppermute | solution.py:704
  12.0 0.0 collective-permute-done.refs_2_
  12.0 0.0 collective-permute-done.1.refs_3_
  12.0 0.0 copy-done.1
  12.0 0.0 copy-start.3
  12.1 0.0 copy-start
  12.1 1.2 %send.1 = (f32[6,64,128]{2,1,0:T(8,128)S(1)}, f32[6,64,128]{2,1,0:T(8,128)S(1)}, f32[34,64,128]{2,1,0:T(8,128)S(1)}, bf16[2048,512]{1,0:T(8,128)(2,1)S(1)}, f32[...) custom-call(f32[32,64,128]{2,1,0:T(8,128)S(1)} %get-tuple-element.24.refs_0_, ...), custom_call_target="tpu_custom_call" | custom-call | tf_op jit(solution)/shard_map/send/pallas_call | solution.py:731
  13.3 2.4 %collective-permute-start.4 = (f32[6,64,128]{2,1,0:T(8,128)S(1)}, f32[6,64,128]{2,1,0:T(8,128)S(1)}, u32[]{:S(2)}, u32[]{:S(2)}) collective-permute-start(f32[6,64,128]{2,1,0:T(8,128)S(1)} %get-tuple-element.35), channel_id=1, source_target_pairs={{0,4},{4,0},{8,12},{12,8},{16,20},{20,16},{24,28},{28,24},{1,5},{5... | collective-permute-start | bytes 589832 | tf_op jit(solution)/shard_map/ppermute | solution.py:704
  15.7 1.9 %collective-permute-start.5 = (f32[6,64,128]{2,1,0:T(8,128)S(1)}, f32[6,64,128]{2,1,0:T(8,128)S(1)}, u32[]{:S(2)}, u32[]{:S(2)}) collective-permute-start(f32[6,64,128]{2,1,0:T(8,128)S(1)} %get-tuple-element.36), channel_id=1, source_target_pairs={{4,8},{8,4},{12,16},{16,12},{20,24},{24,20},{5,9},{9,5},{13,17},{1... | collective-permute-start | bytes 589832 | tf_op jit(solution)/shard_map/ppermute | solution.py:704
  17.6 0.0 copy-done.3
  17.7 1.3 %collective-permute-start.6 = (f32[1,64,128]{2,1,0:T(8,128)S(1)}, f32[1,64,128]{2,1,0:T(8,128)S(1)}, u32[]{:S(2)}, u32[]{:S(2)}) collective-permute-start(f32[1,64,128]{2,1,0:T(8,128)S(1)} %get-tuple-element.37), channel_id=1, source_target_pairs={{0,8},{8,0},{4,12},{12,4},{16,24},{24,16},{20,28},{28,20},{1,9},{9... | collective-permute-start | bytes 98312 | tf_op jit(solution)/shard_map/ppermute | solution.py:704
  18.9 0.0 collective-permute-done.2.refs_3_
  19.0 1.9 %collective-permute-start.7 = (f32[1,64,128]{2,1,0:T(8,128)S(1)}, f32[1,64,128]{2,1,0:T(8,128)S(1)}, u32[]{:S(2)}, u32[]{:S(2)}) collective-permute-start(f32[1,64,128]{2,1,0:T(8,128)S(1)} %get-tuple-element.38), channel_id=1, source_target_pairs={{8,16},{16,8},{12,20},{20,12},{9,17},{17,9},{13,21},{21,13},{10,18... | collective-permute-start | bytes 98312 | tf_op jit(solution)/shard_map/ppermute | solution.py:704
  20.9 0.1 pad_maximum_fusion.refs_6_.refs_10_
  21.0 0.0 copy-done
  21.0 2.8 %local.1 = (f32[17,64,256]{2,1,0:T(8,128)S(1)}, f32[17,64,256]{2,1,0:T(8,128)S(1)}, f32[38,64,128]{2,1,0:T(8,128)S(1)}) custom-call(f32[32,64,384]{2,1,0:T(8,128)S(1)} %get-tuple-element.23.refs_1_.refs_0_, bf16[2048,512]{1,0:T(8,128)(2,1)S(1)} %get-tuple-element.27.refs_1_, f32[32,64,128]{2,1,0:T(8,128)S(1)} %get-tuple-element.28.refs_2_, ...), custom_call_target="tpu_custom_call" | custom-call | tf_op jit(solution)/shard_map/local/pallas_call | solution.py:731
  23.9 0.0 collective-permute-done.3.refs_4_
  23.9 0.0 collective-permute-done.6.refs_7_
  23.9 0.0 collective-permute-done.7.refs_8_
  23.9 1.7 %collective-permute-done.4.refs_5_ = f32[6,64,128]{2,1,0:T(8,128)S(1)} collective-permute-done((f32[6,64,128]{2,1,0:T(8,128)S(1)}, f32[6,64,128]{2,1,0:T(8,128)S(1)}, u32[]{:S(2)}, u32[]{:S(2)}) %collective-permute-start.4) | collective-permute-done | bytes 196640 | tf_op jit(solution)/shard_map/ppermute | solution.py:704
  25.6 0.0 collective-permute-done.5.refs_6_
  25.6 2.8 %final.1 = f32[64,32,256]{2,1,0:T(8,128)} custom-call(f32[17,64,256]{2,1,0:T(8,128)S(1)} %get-tuple-element.30.refs_0_, f32[17,64,256]{2,1,0:T(8,128)S(1)} %get-tuple-element.31.refs_1_, f32[38,64,128]{2,1,0:T(8,128)S(1)} %get-tuple-element.32.refs_2_, f32[5,64,128]{2,1,0:T(8,128)S(1)} %collective-permute-done.2.refs_3_, ...), custom_call_target="tpu_custom_call" | custom-call | tf_op jit(solution)/shard_map/final/pallas_call | solution.py:731
  (1 shorter events, 0.0 us)
Async XLA Ops:
  0.0 7.4 %copy-start.2 = (bf16[3,256,512]{2,1,0:T(8,128)(2,1)S(1)}, bf16[3,256,512]{2,1,0:T(8,128)(2,1)}, u32[]{:S(2)}) copy-start(bf16[3,256,512]{2,1,0:T(8,128)(2,1)} %constant.10.clone.refs_1_) | copy-start | bytes 2359300
  3.6 8.4 %copy-start.1 = (bf16[256,512]{1,0:T(8,128)(2,1)S(1)}, bf16[256,512]{1,0:T(8,128)(2,1)}, u32[]{:S(2)}) copy-start(bf16[256,512]{1,0:T(8,128)(2,1)} %constant.14.clone.refs_4_) | copy-start | bytes 786436
  3.6 8.4 %collective-permute-start = (f32[4,64,128]{2,1,0:T(8,128)S(1)}, f32[4,64,128]{2,1,0:T(8,128)S(1)}, u32[]{:S(2)}, u32[]{:S(2)}) collective-permute-start(f32[4,64,128]{2,1,0:T(8,128)S(1)} %get-tuple-element.25), channel_id=1, source_target_pairs={{0,1},{1,0},{2,3},{3,2},{4,5},{5,4},{6,7},{7,6},{8,9},{9,8},{10,11... | collective-permute-start | bytes 393224 | tf_op jit(solution)/shard_map/ppermute | solution.py:704
  4.3 7.7 %collective-permute-start.1 = (f32[4,64,128]{2,1,0:T(8,128)S(1)}, f32[4,64,128]{2,1,0:T(8,128)S(1)}, u32[]{:S(2)}, u32[]{:S(2)}) collective-permute-start(f32[4,64,128]{2,1,0:T(8,128)S(1)} %get-tuple-element.26), channel_id=1, source_target_pairs={{1,2},{2,1},{5,6},{6,5},{9,10},{10,9},{13,14},{14,13},{17,18},{18,... | collective-permute-start | bytes 393224 | tf_op jit(solution)/shard_map/ppermute | solution.py:704
  8.7 10.3 %collective-permute-start.2 = (f32[5,64,128]{2,1,0:T(8,128)S(1)}, f32[5,64,128]{2,1,0:T(8,128)S(1)}, u32[]{:S(2)}, u32[]{:S(2)}) collective-permute-start(f32[5,64,128]{2,1,0:T(8,128)S(1)} %get-tuple-element.33), channel_id=1, source_target_pairs={{0,4},{4,0},{8,12},{12,8},{16,20},{20,16},{24,28},{28,24},{1,5},{5... | collective-permute-start | bytes 491528 | tf_op jit(solution)/shard_map/ppermute | solution.py:704
  10.0 13.9 %collective-permute-start.3 = (f32[5,64,128]{2,1,0:T(8,128)S(1)}, f32[5,64,128]{2,1,0:T(8,128)S(1)}, u32[]{:S(2)}, u32[]{:S(2)}) collective-permute-start(f32[5,64,128]{2,1,0:T(8,128)S(1)} %get-tuple-element.34), channel_id=1, source_target_pairs={{4,8},{8,4},{12,16},{16,12},{20,24},{24,20},{5,9},{9,5},{13,17},{1... | collective-permute-start | bytes 491528 | tf_op jit(solution)/shard_map/ppermute | solution.py:704
  12.0 5.6 %copy-start.3 = (f32[16,32,32]{2,1,0:T(8,128)S(1)}, f32[16,32,32]{2,1,0:T(8,128)}, u32[]{:S(2)}) copy-start(f32[16,32,32]{2,1,0:T(8,128)} %param.8) | copy-start | bytes 196612
  12.1 9.0 %copy-start = (bf16[3,512,256]{2,1,0:T(8,128)(2,1)S(1)}, bf16[3,512,256]{2,1,0:T(8,128)(2,1)}, u32[]{:S(2)}) copy-start(bf16[3,512,256]{2,1,0:T(8,128)(2,1)} %constant.13.clone.refs_5_.refs_9_) | copy-start | bytes 2359300
  13.3 12.3 %collective-permute-start.4 = (f32[6,64,128]{2,1,0:T(8,128)S(1)}, f32[6,64,128]{2,1,0:T(8,128)S(1)}, u32[]{:S(2)}, u32[]{:S(2)}) collective-permute-start(f32[6,64,128]{2,1,0:T(8,128)S(1)} %get-tuple-element.35), channel_id=1, source_target_pairs={{0,4},{4,0},{8,12},{12,8},{16,20},{20,16},{24,28},{28,24},{1,5},{5... | collective-permute-start | bytes 589832 | tf_op jit(solution)/shard_map/ppermute | solution.py:704
  15.7 9.9 %collective-permute-start.5 = (f32[6,64,128]{2,1,0:T(8,128)S(1)}, f32[6,64,128]{2,1,0:T(8,128)S(1)}, u32[]{:S(2)}, u32[]{:S(2)}) collective-permute-start(f32[6,64,128]{2,1,0:T(8,128)S(1)} %get-tuple-element.36), channel_id=1, source_target_pairs={{4,8},{8,4},{12,16},{16,12},{20,24},{24,20},{5,9},{9,5},{13,17},{1... | collective-permute-start | bytes 589832 | tf_op jit(solution)/shard_map/ppermute | solution.py:704
  17.7 6.2 %collective-permute-start.6 = (f32[1,64,128]{2,1,0:T(8,128)S(1)}, f32[1,64,128]{2,1,0:T(8,128)S(1)}, u32[]{:S(2)}, u32[]{:S(2)}) collective-permute-start(f32[1,64,128]{2,1,0:T(8,128)S(1)} %get-tuple-element.37), channel_id=1, source_target_pairs={{0,8},{8,0},{4,12},{12,4},{16,24},{24,16},{20,28},{28,20},{1,9},{9... | collective-permute-start | bytes 98312 | tf_op jit(solution)/shard_map/ppermute | solution.py:704
  19.0 4.9 %collective-permute-start.7 = (f32[1,64,128]{2,1,0:T(8,128)S(1)}, f32[1,64,128]{2,1,0:T(8,128)S(1)}, u32[]{:S(2)}, u32[]{:S(2)}) collective-permute-start(f32[1,64,128]{2,1,0:T(8,128)S(1)} %get-tuple-element.38), channel_id=1, source_target_pairs={{8,16},{16,8},{12,20},{20,12},{9,17},{17,9},{13,21},{21,13},{10,18... | collective-permute-start | bytes 98312 | tf_op jit(solution)/shard_map/ppermute | solution.py:704

commit v3 on v2

--- a/solution.py
+++ b/solution.py
@@ -7,6 +7,7 @@
 from jax.experimental import pallas as pl
 from jax.experimental.pallas import tpu as pltpu
 from jax.sharding import PartitionSpec as P
+
 
 LEVELS = 5
 TILE = 128
@@ -173,18 +174,20 @@
     return edge, (kind, lax.rem(iy, 2), lax.rem(ix, 2), lax.rem(ix // 2, 2))
 
 
-def first_kernel(nx, edge_ref, var_ref, x_ref, ehi_ref, elo_ref, xhl, yc_ref, one_ref, two_ref, xt, e3, sems):
+def first_kernel(nx, edge_ref, var_ref, x_ref, ehi_ref, elo_ref, a_ref,
+                 xhl, yc_ref, one_ref, two_ref, rows_ref, xt, e3, a2, low, high, sems):
     g, ny = xt.shape[1], xt.shape[3]
     consts = [
         pltpu.make_async_copy(ref.at[var_ref[0]], e3.at[pl.ds(j * ny, ny)], sems.at[nx + j])
-        for j, ref in enumerate((ehi_ref, ehi_ref, elo_ref))
+        for j, ref in ((0, ehi_ref), (2, elo_ref))
     ]
+    late = pltpu.make_async_copy(a_ref.at[var_ref[0], :, pl.ds(0, ny)], a2.at[pl.ds(0, ny)], sems.at[nx + 3])
     per = TILE // SLOT
     copies = [
         pltpu.make_async_copy(x_ref.at[:, pl.ds(r, per)], xt.at[r // per], sems.at[r // per])
         for r in range(0, nx, per)
     ]
-    for copy in copies[:1] + consts + copies[1:]:
+    for copy in copies[:1] + consts + copies[1:] + [late]:
         copy.start()
     odd = var_ref[1] == 1
     for r in range(0, nx, per):
@@ -199,6 +202,7 @@
             if q == 0:
                 for copy in consts:
                     copy.wait()
+                e3[ny : 2 * ny] = e3[0:ny]
             res = dot(xhl[q * g : (q + 4) * g], e3[...])
             for i in range(q, q + 4):
                 part = res[(i - q) * g : (i - q + 1) * g]
@@ -211,22 +215,33 @@
                 down = jnp.where(group, b, 0.0 if down is None else down)
         one_ref[r // per] = jnp.where(odd, down, up)
         two_ref[r // per] = jnp.where(odd, up, down)
-
-
-def main_kernel(nx, edge_ref, var_ref, xhl, a_ref, y_ref, one_ref, two_ref, a2):
+    late.wait()
+    a2[ny : 2 * ny] = a2[0:ny]
+    count, top = low.shape[0], nx - high.shape[0]
+    low[...] = dot(xhl[0 : count * g, 0 : 2 * ny], a2[...]).reshape(low.shape)
+    high[...] = dot(xhl[top * g :, 0 : 2 * ny], a2[...]).reshape(high.shape)
+    lift = Lift(nx, lambda i: low[i], edge_ref, 0, count - 1)
+    begin, then = lift.detail(1, -1), lift.detail(1, 0)
+    last = Lift(nx, lambda i: high[i - top], edge_ref, top, nx - 1).detail(1, (nx >> 1) - 1)
+    for t, value in enumerate((last, begin, then)):
+        rows_ref[2 * t], rows_ref[2 * t + 1] = value[:, 0:TILE], value[:, TILE:]
+
+
+def main_kernel(nx, edge_ref, var_ref, xhl, a_ref, y_ref, a2):
     g, ny = y_ref.shape[1], a_ref.shape[1]
     a2[0:ny], a2[ny : 2 * ny] = a_ref[var_ref[0]], a_ref[var_ref[0]]
     step = 4
     for r in range(0, nx, step):
         res = dot(xhl[r * g : (r + step) * g, 0 : 2 * ny], a2[...])
         y_ref[r : r + step] = res[:, 0 : y_ref.shape[2]].reshape(step, g, y_ref.shape[2])
-    lift = Lift(nx, lambda i: y_ref[i, :, 0:ny], edge_ref)
-    zero = jnp.zeros((g, TILE), F32)
-    top, begin, then = lift.detail(1, (nx >> 1) - 1), lift.detail(1, -1), lift.detail(1, 0)
-    row = lift.smooth(1, 0)
-    up = [top[:, 0:TILE], top[:, TILE:], zero, zero, zero]
-    down = [begin[:, 0:TILE], begin[:, TILE:], then[:, 0:TILE], then[:, TILE:], row[:, TILE:]]
-    to_pairs(var_ref[2], up, down, one_ref, two_ref)
+
+
+def relay_kernel(edge_ref, var_ref, rows_ref, up_ref, down_ref, one_ref, two_ref):
+    up, down = [up_ref[...]], [down_ref[...]]
+    zero = jnp.zeros(up_ref.shape, F32)
+    up += [rows_ref[0], rows_ref[1], zero, zero]
+    down += [rows_ref[t] for t in range(2, 6)]
+    to_pairs(var_ref[3], up, down, one_ref, two_ref)
 
 
 def to_pairs(odd, up, down, one_ref, two_ref):
@@ -312,15 +327,10 @@
 
 def send_kernel(nx, far, edge_ref, var_ref, yc_ref, ym_ref, one_ref, two_ref, p_ref, *rest):
     to_one_ref, to_two_ref, cc_ref, z, y2_ref = rest[:5]
-    rest = rest[5:]
-    if far:
-        far_one_ref, far_two_ref = rest[:2]
-        rest = rest[2:]
-    yc, yl, yh, p2 = rest
+    far_up_ref, far_down_ref, yc, yl, yh, p2 = rest[5:]
     g = yc.shape[1]
     mains = ym_ref.shape[2]
     ny = mains - TILE
-    half = ny // 2
     _, spans = lane_plan(ny)
     n1, n2 = nx >> 1, nx >> 2
     n = 2 * TILE
@@ -353,7 +363,7 @@
     second = Lift(nx, lambda i: y2_ref[i], edge_ref)
     one, two = lift(yl, 0), lift(yh, nx - high)
     fix_up = [two.detail(1, n1 - 1)]
-    fix_down = [one.detail(1, -1), one.detail(1, 0), one.smooth(1, 0)]
+    fix_down = [one.detail(1, -1), one.detail(1, 0)]
     up = [second.detail(2, n2 - 1), second.detail(2, n2), put_fixes(second.smooth(2, n2), fix_up)]
     down = [second.detail(2, -1), second.detail(2, 0), put_fixes(second.smooth(2, 0), fix_down)]
 
@@ -369,11 +379,9 @@
         new = [deep.detail(k, n - 1)] + ([deep.detail(k, n), deep.smooth(k, n)] if k > 1 else [None] * 2)
         acc = [a if v is None else jnp.where(here, v, a) for a, v in zip(acc, new)]
     to_pairs(var_ref[2], up + acc, down + [cc_ref[0], cc_ref[1], cc_ref[n1 + 1]], to_one_ref, to_two_ref)
-    if far:
-        here = in_span(spans[LEVELS])
-        up = jnp.where(here, deep.detail(LEVELS, nx >> LEVELS), 0.0)
-        down = jnp.where(here, deep.detail(LEVELS, -1), 0.0)
-        to_pairs(var_ref[3], [up], [down], far_one_ref, far_two_ref)
+    here = in_span(spans[LEVELS]) if far else lanes() < 0
+    far_up_ref[...] = jnp.where(here, deep.detail(LEVELS, nx >> LEVELS), 0.0)
+    far_down_ref[...] = jnp.where(here, deep.detail(LEVELS, -1), 0.0)
 
 
 def put_fixes(tile, fixes):
@@ -547,11 +555,8 @@
         store(("m2", "s"), 0, some, weigh_m2(r_ref, "s", [m2.smooth(2, i) for i in some]))
 
 
-def final_kernel(nx, far, edge_ref, var_ref, vd_ref, vs_ref, w_ref, e_one, e_two, r_one, r_two, *rest):
-    if far:
-        f_one, f_two = rest[:2]
-        rest = rest[2:]
-    s_ref, r_ref, out_ref, sd, ss, sdeep, zd, zs, zdeep, rows, ot, sem = rest
+def final_kernel(nx, edge_ref, var_ref, vd_ref, vs_ref, w_ref, near, r_one, r_two, f_one, f_two,
+                 s_ref, r_ref, out_ref, sd, ss, sdeep, zd, zs, zdeep, rows, ot, sem):
     g, ny = ot.shape[1], ot.shape[3]
     _, spans = lane_plan(ny)
     plan, _ = weighted_plan(nx)
@@ -568,7 +573,10 @@
         return jnp.where(s_lanes, 0.25 * value, 0.0)
 
     below, above = from_pairs(var_ref[2], r_one, r_two)
-    first_below, first_above = from_pairs(var_ref[2], e_one, e_two)
+    far_below, far_above = from_pairs(var_ref[3], f_one, f_two)
+    odd = var_ref[2] == 1
+    first_below = [jnp.where(odd, near[t], far_below[1 + t]) for t in range(2)]
+    first_above = [jnp.where(odd, far_above[1 + t], near[2 + t]) for t in range(4)]
     c_d = {-1: below[3], 0: below[4], "n-1": above[3], "n": above[4]}
     c_s = {
         0: below[5] + jnp.where(lev1, smooth_c(c_d[-1]), 0.0),
@@ -576,16 +584,14 @@
         "n-1": smooth_c(c_d["n-1"]),
         "n": above[5],
     }
-    if far:
-        (far_below,), (far_above,) = from_pairs(var_ref[3], f_one, f_two)
-        c_d[-1] = c_d[-1] + far_below
-        c_s[0] = c_s[0] + smooth_c(far_below)
-        c_d["n"] = c_d["n"] + far_above
-        c_s["n"] = c_s["n"] + smooth_c(far_above)
-    fixes = [get_fix(below[2], 0)] + [get_fix(above[2], j) for j in range(3)]
+    c_d[-1] = c_d[-1] + far_below[0]
+    c_s[0] = c_s[0] + smooth_c(far_below[0])
+    c_d["n"] = c_d["n"] + far_above[0]
+    c_s["n"] = c_s["n"] + smooth_c(far_above[0])
+    fixes = [get_fix(below[2], 0)] + [get_fix(above[2], j) for j in range(2)]
     a_tiles = [first_below[0] + fixes[0][0], first_above[0] + fixes[1][0], first_above[2] + fixes[2][0]]
     b_tiles = [first_below[1] + fixes[0][1], first_above[1] + fixes[1][1], first_above[3] + fixes[2][1]]
-    s_tiles = [0.25 * b_tiles[0], 0.25 * b_tiles[1], first_above[4] + fixes[3][1]]
+    s_tiles = [0.25 * b_tiles[0], 0.25 * b_tiles[1], 0.25 * b_tiles[2] - 1.75 * b_tiles[1]]
     every = list(range(1, LEVELS + 1))
     got = {}
 
@@ -714,7 +720,7 @@
     far = (nx >> LEVELS) < 2 and gx > 2
     consts = y_constants(ny, gy)
     main_mat, ehi_mat, elo_mat, s_mat, p_mat = (jnp.asarray(t) for t in consts)
-    n1, n2 = nx >> 1, nx >> 2
+    n1 = nx >> 1
     mains = ny + half
 
     r_hi = lax.reduce_precision(band_roots, 8, 7)
@@ -724,7 +730,7 @@
     hbm = pl.BlockSpec(memory_space=pl.ANY)
     vmem = pl.BlockSpec(memory_space=pltpu.VMEM)
 
-    def call(kernel, ins, outs, scratches, name, out_specs=None):
+    def call(kernel, ins, outs, scratches, out_specs=None):
         def body(*refs):
             kernel(*device_place(gx, gy), *refs)
 
@@ -734,47 +740,49 @@
             in_specs=[s for _, s in ins],
             out_specs=out_specs or (vmem,) * len(outs),
             scratch_shapes=scratches,
-            name=name,
             compiler_params=pltpu.CompilerParams(vmem_limit_bytes=VMEM_LIMIT),
         )(*[a for a, _ in ins])
 
     tile = (g, TILE)
     rows3 = control.reshape(g, nx, ny)
     far_hbm = pl.BlockSpec(memory_space=pltpu.HBM)
-    xhl, yc, one, two = call(
+    xhl, yc, one, two, rows = call(
         partial(first_kernel, nx),
-        [(pltpu.with_memory_space_constraint(t, pltpu.HBM), far_hbm) for t in (rows3, ehi_mat, elo_mat)],
-        [((nx * g, 3 * ny), BF), ((nx,) + tile, F32), ((nx // per,) + tile, F32), ((nx // per,) + tile, F32)],
-        [pltpu.VMEM((nx // per, g, per, ny), F32), pltpu.VMEM((3 * ny, 2 * TILE), BF), pltpu.SemaphoreType.DMA((nx + 3,))],
-        "first",
+        [
+            (pltpu.with_memory_space_constraint(t, pltpu.HBM), far_hbm)
+            for t in (rows3, ehi_mat, elo_mat, main_mat)
+        ],
+        [((nx * g, 3 * ny), BF), ((nx,) + tile, F32), ((nx // per,) + tile, F32), ((nx // per,) + tile, F32),
+         ((6,) + tile, F32)],
+        [pltpu.VMEM((nx // per, g, per, ny), F32), pltpu.VMEM((3 * ny, 2 * TILE), BF),
+         pltpu.VMEM((2 * ny, ny), BF), pltpu.VMEM((4, g, ny), F32), pltpu.VMEM((4, g, ny), F32),
+         pltpu.SemaphoreType.DMA((nx + 4,))],
     )
+    near = swap(rows, "gx", 0)
     got_one = swap(one, "gy", 0)
     got_two = swap(two, "gy", 1)
-    ym, one, two = call(
+    (ym,) = call(
         partial(main_kernel, nx),
         [(xhl, vmem), (main_mat, vmem)],
-        [((nx, g, mains), F32), ((5,) + tile, F32), ((5,) + tile, F32)],
+        [((nx, g, mains), F32)],
         [pltpu.VMEM((2 * ny, mains + TILE), BF)],
-        "main",
     )
-    got = [(swap(one, "gx", 0), vmem), (swap(two, "gx", 1), vmem)]
     slots = 2 * n1 + 2
     sent = call(
         partial(send_kernel, nx, far),
         [(yc, vmem), (ym, vmem), (got_one, vmem), (got_two, vmem), (p_mat, vmem)],
         [((6,) + tile, F32), ((6,) + tile, F32), ((slots,) + tile, F32), ((nx * g, 4 * TILE), BF), ((nx,) + tile, F32)]
-        + ([((1,) + tile, F32)] * 2 if far else []),
+        + [(tile, F32)] * 2,
         [
             pltpu.VMEM((nx,) + tile, F32),
             pltpu.VMEM((4,) + tile, F32),
             pltpu.VMEM((4,) + tile, F32),
             pltpu.VMEM((4 * TILE, mains + TILE), BF),
         ],
-        "send",
     )
-    got += [(swap(sent[0], "gx", 0), vmem), (swap(sent[1], "gx", 1), vmem)]
-    if far:
-        got += [(swap(sent[5], "gx", 0, 2), vmem), (swap(sent[6], "gx", 2, 2), vmem)]
+    got = [near, swap(sent[0], "gx", 0), swap(sent[1], "gx", 1)]
+    far_one, far_two = call(relay_kernel, [(t, vmem) for t in (near, sent[5], sent[6])], [((5,) + tile, F32)] * 2, [])
+    got += [swap(far_one, "gx", 0, 2), swap(far_two, "gx", 2, 2)]
 
     _, count = weighted_plan(nx)
     vd, vs, w = call(
@@ -789,11 +797,10 @@
             pltpu.VMEM((6 * TILE, ny), BF),
             pltpu.VMEM((4 * TILE, ny), BF),
         ],
-        "local",
     )
     (out,) = call(
-        partial(final_kernel, nx, far),
-        [(vd, vmem), (vs, vmem), (w, vmem)] + got + [(s_mat, vmem), (roots, vmem)],
+        partial(final_kernel, nx),
+        [(t, vmem) for t in [vd, vs, w] + got + [s_mat, roots]],
         [((g, nx, ny), F32)],
         [
             pltpu.VMEM((6 * TILE, ny), BF),
@@ -806,15 +813,11 @@
             pltpu.VMEM((nx // 8, g, 8, ny), F32),
             pltpu.SemaphoreType.DMA((nx // 8,)),
         ],
-        "final",
         (hbm,),
     )
     return out.reshape(control.shape)
 
 
 def solution(mesh):
-    in_specs = (P(None, None, "gx", "gy"), P())
-    out_specs = P(None, None, "gx", "gy")
-    return jax.shard_map(
-        per_device, mesh=mesh, in_specs=in_specs, out_specs=out_specs, check_vma=False
-    )
+    spec = P(None, None, "gx", "gy")
+    return jax.shard_map(per_device, mesh=mesh, in_specs=(spec, P()), out_specs=spec, check_vma=False)

time: 28.6 us -> 28.7 us (level)
  the two profiles are of different devices: /device:TPU:17 before, /device:TPU:20 now
where the time goes in v3:
time: 28.7 us; the launch traced here: 28.5 us
  Pallas kernels  12 us (42%)
  starting transfers between devices  11.5 us (40%)
  waiting for transfers between devices  4.66 us (16%)
    pallas_call x6, Pallas kernels, call(): pl.pallas_call(body, out_shape=tuple((jax.ShapeDtypeStruct(*s) for s in o...  12 us
    ppermute x7, starting transfers between devices, swap(): lax.ppermute(value, axis, [p for i in starts for p in ((i, i + step), (i...  11.5 us
    ppermute x7, waiting for transfers between devices, swap(): lax.ppermute(value, axis, [p for i in starts for p in ((i, i + step), (i...  4.66 us
  transfers between devices with their start and end apart: 7, of which 3 were waited for; matrix products, arithmetic and copies ran while one was open for 1% of the time, Pallas kernels for 19%

profile of v3, /device:TPU:20, one launch (start us, length us, event | category | flops | bytes accessed | tf_op | source)
XLA Modules:
  0.0 28.5 jit_solution(13883352150158414850)
XLA Ops:
  0.0 0.0 copy-start.1
  0.0 3.9 %shard_map.73 = (bf16[2048,768]{1,0:T(8,128)(2,1)S(1)}, f32[32,64,128]{2,1,0:T(8,128)S(1)}, f32[4,64,128]{2,1,0:T(8,128)S(1)}, f32[4,64,128]{2,1,0:T(8,128)S(1)}, f32[6,64,128]{2,1,0:T(8,128)S(1)}) custom-call(f32[64,32,256]{2,1,0:T(8,128)} %bitcast.2, bf16[3,256,256]{2,1,0:T(8,128)(2,1)} %constant.11.clone.refs_1_, ...), custom_call_target="tpu_custom_call" | custom-call | tf_op jit(solution)/shard_map/pallas_call | solution.py:737
  3.9 1.6 %collective-permute-start.2 = (f32[6,64,128]{2,1,0:T(8,128)S(1)}, f32[6,64,128]{2,1,0:T(8,128)S(1)}, u32[]{:S(2)}, u32[]{:S(2)}) collective-permute-start(f32[6,64,128]{2,1,0:T(8,128)S(1)} %get-tuple-element.32), channel_id=1, source_target_pairs={{0,4},{4,0},{8,12},{12,8},{16,20},{20,16},{24,28},{28,24},{1,5},{5... | collective-permute-start | bytes 589832 | tf_op jit(solution)/shard_map/ppermute | solution.py:710
  5.4 0.0 collective-permute-start
  5.4 2.5 %collective-permute-start.1 = (f32[4,64,128]{2,1,0:T(8,128)S(1)}, f32[4,64,128]{2,1,0:T(8,128)S(1)}, u32[]{:S(2)}, u32[]{:S(2)}) collective-permute-start(f32[4,64,128]{2,1,0:T(8,128)S(1)} %get-tuple-element.25), channel_id=1, source_target_pairs={{1,2},{2,1},{5,6},{6,5},{9,10},{10,9},{13,14},{14,13},{17,18},{18,... | collective-permute-start | bytes 393224 | tf_op jit(solution)/shard_map/ppermute | solution.py:710
  8.0 0.0 copy-done.1
  8.0 0.0 copy-start.2
  8.0 1.3 %shard_map.74.refs_1_.refs_0_ = f32[32,64,384]{2,1,0:T(8,128)S(1)} custom-call(bf16[2048,768]{1,0:T(8,128)(2,1)S(1)} %get-tuple-element.22.refs_0_, bf16[3,256,512]{2,1,0:T(8,128)(2,1)S(1)} %copy-done.1), custom_call_target="tpu_custom_call" | custom-call | tf_op jit(solution)/shard_map/pallas_call | solution.py:737
  9.2 0.0 collective-permute-done.refs_2_
  9.3 2.4 %collective-permute-done.1.refs_3_ = f32[4,64,128]{2,1,0:T(8,128)S(1)} collective-permute-done((f32[4,64,128]{2,1,0:T(8,128)S(1)}, f32[4,64,128]{2,1,0:T(8,128)S(1)}, u32[]{:S(2)}, u32[]{:S(2)}) %collective-permute-start.1) | collective-permute-done | bytes 131104 | tf_op jit(solution)/shard_map/ppermute | solution.py:710
  11.7 0.0 copy-done.2
  11.7 0.0 copy-start.3
  11.7 0.0 copy-start
  11.7 1.2 %shard_map.75 = (f32[6,64,128]{2,1,0:T(8,128)S(1)}, f32[6,64,128]{2,1,0:T(8,128)S(1)}, f32[34,64,128]{2,1,0:T(8,128)S(1)}, bf16[2048,512]{1,0:T(8,128)(2,1)S(1)}...) custom-call(f32[32,64,128]{2,1,0:T(8,128)S(1)} %get-tuple-element.23.refs_0_, ...), custom_call_target="tpu_custom_call" | custom-call | tf_op jit(solution)/shard_map/pallas_call | solution.py:737
  12.9 0.6 %collective-permute-start.3 = (f32[6,64,128]{2,1,0:T(8,128)S(1)}, f32[6,64,128]{2,1,0:T(8,128)S(1)}, u32[]{:S(2)}, u32[]{:S(2)}) collective-permute-start(f32[6,64,128]{2,1,0:T(8,128)S(1)} %get-tuple-element.33), channel_id=1, source_target_pairs={{0,4},{4,0},{8,12},{12,8},{16,20},{20,16},{24,28},{28,24},{1,5},{5... | collective-permute-start | bytes 589832 | tf_op jit(solution)/shard_map/ppermute | solution.py:710
  13.5 3.3 %collective-permute-start.4 = (f32[6,64,128]{2,1,0:T(8,128)S(1)}, f32[6,64,128]{2,1,0:T(8,128)S(1)}, u32[]{:S(2)}, u32[]{:S(2)}) collective-permute-start(f32[6,64,128]{2,1,0:T(8,128)S(1)} %get-tuple-element.34), channel_id=1, source_target_pairs={{4,8},{8,4},{12,16},{16,12},{20,24},{24,20},{5,9},{9,5},{13,17},{1... | collective-permute-start | bytes 589832 | tf_op jit(solution)/shard_map/ppermute | solution.py:710
  16.8 0.0 collective-permute-done.2.refs_0_.refs_3_
  16.9 1.6 %collective-permute-start.5 = (f32[5,64,128]{2,1,0:T(8,128)S(1)}, f32[5,64,128]{2,1,0:T(8,128)S(1)}, u32[]{:S(2)}, u32[]{:S(2)}) collective-permute-start(f32[5,64,128]{2,1,0:T(8,128)S(1)} %get-tuple-element.37), channel_id=1, source_target_pairs={{0,8},{8,0},{4,12},{12,4},{16,24},{24,16},{20,28},{28,20},{1,9},{9... | collective-permute-start | bytes 491528 | tf_op jit(solution)/shard_map/ppermute | solution.py:710
  18.5 1.9 %collective-permute-start.6 = (f32[5,64,128]{2,1,0:T(8,128)S(1)}, f32[5,64,128]{2,1,0:T(8,128)S(1)}, u32[]{:S(2)}, u32[]{:S(2)}) collective-permute-start(f32[5,64,128]{2,1,0:T(8,128)S(1)} %get-tuple-element.38), channel_id=1, source_target_pairs={{8,16},{16,8},{12,20},{20,12},{9,17},{17,9},{13,21},{21,13},{10,18... | collective-permute-start | bytes 491528 | tf_op jit(solution)/shard_map/ppermute | solution.py:710
  20.4 0.0 copy-done.3
  20.5 0.1 pad_maximum_fusion.refs_6_.refs_9_
  20.6 0.0 copy-done
  20.6 2.8 %shard_map.76 = (f32[17,64,256]{2,1,0:T(8,128)S(1)}, f32[17,64,256]{2,1,0:T(8,128)S(1)}, f32[38,64,128]{2,1,0:T(8,128)S(1)}) custom-call(f32[32,64,384]{2,1,0:T(8,128)S(1)} %shard_map.74.refs_1_.refs_0_, bf16[2048,512]{1,0:T(8,128)(2,1)S(1)} %get-tuple-element.26.refs_1_, f32[32,64,128]{2,1,0:T(8,128)S(1)} %get-tuple-element.27.refs_2_, ...), custom_call_target="tpu_custom_call" | custom-call | tf_op jit(solution)/shard_map/pallas_call | solution.py:737
  23.5 0.0 collective-permute-done.3.refs_4_
  23.5 0.0 collective-permute-done.4.refs_5_
  23.5 0.3 collective-permute-done.5.refs_6_
  23.8 2.0 %collective-permute-done.6.refs_7_ = f32[5,64,128]{2,1,0:T(8,128)S(1)} collective-permute-done((f32[5,64,128]{2,1,0:T(8,128)S(1)}, f32[5,64,128]{2,1,0:T(8,128)S(1)}, u32[]{:S(2)}, u32[]{:S(2)}) %collective-permute-start.6) | collective-permute-done | bytes 163872 | tf_op jit(solution)/shard_map/ppermute | solution.py:710
  25.7 2.8 %shard_map.78 = f32[64,32,256]{2,1,0:T(8,128)} custom-call(f32[17,64,256]{2,1,0:T(8,128)S(1)} %get-tuple-element.29.refs_0_, f32[17,64,256]{2,1,0:T(8,128)S(1)} %get-tuple-element.30.refs_1_, f32[38,64,128]{2,1,0:T(8,128)S(1)} %get-tuple-element.31.refs_2_, f32[6,64,128]{2,1,0:T(8,128)S(1)} %collective-permute-done.2.refs_0_.refs_3_, ...), custom_call_target="tpu_custom_call" | custom-call | tf_op jit(solution)/shard_map/pallas_call | solution.py:737
  (2 shorter events, 0.1 us)
Async XLA Ops:
  0.0 8.0 %copy-start.1 = (bf16[3,256,512]{2,1,0:T(8,128)(2,1)S(1)}, bf16[3,256,512]{2,1,0:T(8,128)(2,1)}, u32[]{:S(2)}) copy-start(bf16[3,256,512]{2,1,0:T(8,128)(2,1)} %constant.10.clone.refs_3_.refs_1_) | copy-start | bytes 2359300
  3.9 12.9 %collective-permute-start.2 = (f32[6,64,128]{2,1,0:T(8,128)S(1)}, f32[6,64,128]{2,1,0:T(8,128)S(1)}, u32[]{:S(2)}, u32[]{:S(2)}) collective-permute-start(f32[6,64,128]{2,1,0:T(8,128)S(1)} %get-tuple-element.32), channel_id=1, source_target_pairs={{0,4},{4,0},{8,12},{12,8},{16,20},{20,16},{24,28},{28,24},{1,5},{5... | collective-permute-start | bytes 589832 | tf_op jit(solution)/shard_map/ppermute | solution.py:710
  5.4 3.8 %collective-permute-start = (f32[4,64,128]{2,1,0:T(8,128)S(1)}, f32[4,64,128]{2,1,0:T(8,128)S(1)}, u32[]{:S(2)}, u32[]{:S(2)}) collective-permute-start(f32[4,64,128]{2,1,0:T(8,128)S(1)} %get-tuple-element.24), channel_id=1, source_target_pairs={{0,1},{1,0},{2,3},{3,2},{4,5},{5,4},{6,7},{7,6},{8,9},{9,8},{10,11... | collective-permute-start | bytes 393224 | tf_op jit(solution)/shard_map/ppermute | solution.py:710
  5.4 6.3 %collective-permute-start.1 = (f32[4,64,128]{2,1,0:T(8,128)S(1)}, f32[4,64,128]{2,1,0:T(8,128)S(1)}, u32[]{:S(2)}, u32[]{:S(2)}) collective-permute-start(f32[4,64,128]{2,1,0:T(8,128)S(1)} %get-tuple-element.25), channel_id=1, source_target_pairs={{1,2},{2,1},{5,6},{6,5},{9,10},{10,9},{13,14},{14,13},{17,18},{18,... | collective-permute-start | bytes 393224 | tf_op jit(solution)/shard_map/ppermute | solution.py:710
  8.0 3.7 %copy-start.2 = (bf16[256,512]{1,0:T(8,128)(2,1)S(1)}, bf16[256,512]{1,0:T(8,128)(2,1)}, u32[]{:S(2)}) copy-start(bf16[256,512]{1,0:T(8,128)(2,1)} %constant.14.clone.refs_4_) | copy-start | bytes 786436
  11.7 8.7 %copy-start.3 = (f32[16,32,32]{2,1,0:T(8,128)S(1)}, f32[16,32,32]{2,1,0:T(8,128)}, u32[]{:S(2)}) copy-start(f32[16,32,32]{2,1,0:T(8,128)} %param.8) | copy-start | bytes 196612
  11.7 8.9 %copy-start = (bf16[3,512,256]{2,1,0:T(8,128)(2,1)S(1)}, bf16[3,512,256]{2,1,0:T(8,128)(2,1)}, u32[]{:S(2)}) copy-start(bf16[3,512,256]{2,1,0:T(8,128)(2,1)} %constant.13.clone.refs_5_.refs_8_) | copy-start | bytes 2359300
  12.9 10.6 %collective-permute-start.3 = (f32[6,64,128]{2,1,0:T(8,128)S(1)}, f32[6,64,128]{2,1,0:T(8,128)S(1)}, u32[]{:S(2)}, u32[]{:S(2)}) collective-permute-start(f32[6,64,128]{2,1,0:T(8,128)S(1)} %get-tuple-element.33), channel_id=1, source_target_pairs={{0,4},{4,0},{8,12},{12,8},{16,20},{20,16},{24,28},{28,24},{1,5},{5... | collective-permute-start | bytes 589832 | tf_op jit(solution)/shard_map/ppermute | solution.py:710
  13.5 10.0 %collective-permute-start.4 = (f32[6,64,128]{2,1,0:T(8,128)S(1)}, f32[6,64,128]{2,1,0:T(8,128)S(1)}, u32[]{:S(2)}, u32[]{:S(2)}) collective-permute-start(f32[6,64,128]{2,1,0:T(8,128)S(1)} %get-tuple-element.34), channel_id=1, source_target_pairs={{4,8},{8,4},{12,16},{16,12},{20,24},{24,20},{5,9},{9,5},{13,17},{1... | collective-permute-start | bytes 589832 | tf_op jit(solution)/shard_map/ppermute | solution.py:710
  16.9 6.9 %collective-permute-start.5 = (f32[5,64,128]{2,1,0:T(8,128)S(1)}, f32[5,64,128]{2,1,0:T(8,128)S(1)}, u32[]{:S(2)}, u32[]{:S(2)}) collective-permute-start(f32[5,64,128]{2,1,0:T(8,128)S(1)} %get-tuple-element.37), channel_id=1, source_target_pairs={{0,8},{8,0},{4,12},{12,4},{16,24},{24,16},{20,28},{28,20},{1,9},{9... | collective-permute-start | bytes 491528 | tf_op jit(solution)/shard_map/ppermute | solution.py:710
  18.5 7.2 %collective-permute-start.6 = (f32[5,64,128]{2,1,0:T(8,128)S(1)}, f32[5,64,128]{2,1,0:T(8,128)S(1)}, u32[]{:S(2)}, u32[]{:S(2)}) collective-permute-start(f32[5,64,128]{2,1,0:T(8,128)S(1)} %get-tuple-element.38), channel_id=1, source_target_pairs={{8,16},{16,8},{12,20},{20,12},{9,17},{17,9},{13,21},{21,13},{10,18... | collective-permute-start | bytes 491528 | tf_op jit(solution)/shard_map/ppermute | solution.py:710

commit v4 on v3

--- a/solution.py
+++ b/solution.py
@@ -51,6 +51,7 @@
 
 
 SLOT = 16
+REACH = 64
 
 
 def edge_lanes(side):
@@ -133,20 +134,22 @@
         kinds = [(False, False)]
     else:
         kinds = [(False, True), (True, True), (True, False)]
-    main, e_hi, e_lo, back = [], [], [], []
+    main, main_lo, e_hi, e_lo, back = [], [], [], [], []
     for below, above in kinds:
         ana, syn, send = y_matrices(ny, below, above)
-        hi, lo = split_np(np.concatenate([ana["m1"], ana["m2"], np.zeros((ny, TILE))], 1))
-        assert not np.any(lo.astype(np.float32))
+        hi, lo = split_np(np.concatenate([ana["m1"], ana["m2"], ana["c"]], 1))
+        assert not np.any(lo[:, : ny + ny // 2].astype(np.float32))
         main.append(hi)
+        main_lo.append(lo[:, ny + ny // 2 :])
         edge = np.tile(np.concatenate([send[1], send[-1]], 1), (1, TILE // (2 * SLOT)))
-        hi, lo = split_np(np.concatenate([ana["c"], edge], 1))
+        assert not np.any(edge[REACH : ny - REACH])
+        hi, lo = split_np(np.concatenate([edge[:REACH], edge[ny - REACH :]], 0))
         e_hi.append(hi)
         e_lo.append(lo)
         hi, lo = split_np(np.concatenate([syn["m1"], syn["m2"], syn["c"]], 0))
         assert not np.any(lo.astype(np.float32))
         back.append(hi)
-    return np.stack(main), np.stack(e_hi), np.stack(e_lo), np.stack(back), split_np(y_received(ny))[0]
+    return *(np.stack(t) for t in (main, main_lo, e_hi, e_lo, back)), split_np(y_received(ny))[0]
 
 
 def split(value):
@@ -175,10 +178,10 @@
 
 
 def first_kernel(nx, edge_ref, var_ref, x_ref, ehi_ref, elo_ref, a_ref,
-                 xhl, yc_ref, one_ref, two_ref, rows_ref, xt, e3, a2, low, high, sems):
+                 xhl, one_ref, two_ref, rows_ref, xt, e3, a2, ends, low, high, sems):
     g, ny = xt.shape[1], xt.shape[3]
     consts = [
-        pltpu.make_async_copy(ref.at[var_ref[0]], e3.at[pl.ds(j * ny, ny)], sems.at[nx + j])
+        pltpu.make_async_copy(ref.at[var_ref[0]], e3.at[pl.ds(j * TILE, TILE)], sems.at[nx + j])
         for j, ref in ((0, ehi_ref), (2, elo_ref))
     ]
     late = pltpu.make_async_copy(a_ref.at[var_ref[0], :, pl.ds(0, ny)], a2.at[pl.ds(0, ny)], sems.at[nx + 3])
@@ -190,24 +193,14 @@
     for copy in copies[:1] + consts + copies[1:] + [late]:
         copy.start()
     odd = var_ref[1] == 1
-    for r in range(0, nx, per):
+    low_half = lanes() < REACH
+
+    def edges(r):
         up = down = None
-        copies[r // per].wait()
-        block = jnp.swapaxes(xt[r // per], 0, 1)
         for q in range(r, r + per, 4):
+            res = dot(ends[q * g : (q + 4) * g], e3[...])
             for i in range(q, q + 4):
-                rows = slice(i * g, (i + 1) * g)
-                hi, lo = split(block[i - r])
-                xhl[rows, 0:ny], xhl[rows, ny : 2 * ny], xhl[rows, 2 * ny : 3 * ny] = hi, lo, hi
-            if q == 0:
-                for copy in consts:
-                    copy.wait()
-                e3[ny : 2 * ny] = e3[0:ny]
-            res = dot(xhl[q * g : (q + 4) * g], e3[...])
-            for i in range(q, q + 4):
-                part = res[(i - q) * g : (i - q + 1) * g]
-                yc_ref[i] = part[:, 0:TILE]
-                plain = part[:, TILE : 2 * TILE]
+                plain = res[(i - q) * g : (i - q + 1) * g]
                 turned = pltpu.roll(plain, SLOT, 1)
                 group = lanes() // SLOT == i - r
                 a, b = (plain, turned) if i % 2 == 0 else (turned, plain)
@@ -215,6 +208,22 @@
                 down = jnp.where(group, b, 0.0 if down is None else down)
         one_ref[r // per] = jnp.where(odd, down, up)
         two_ref[r // per] = jnp.where(odd, up, down)
+
+    for r in range(0, nx, per):
+        copies[r // per].wait()
+        if r == per:
+            for copy in consts:
+                copy.wait()
+            e3[TILE : 2 * TILE] = e3[0:TILE]
+        block = jnp.swapaxes(xt[r // per], 0, 1)
+        for i in range(r, r + per):
+            rows = slice(i * g, (i + 1) * g)
+            hi, lo = split(block[i - r])
+            xhl[rows, 0:ny], xhl[rows, ny : 2 * ny] = hi, lo
+            hi, lo = (jnp.where(low_half, t[:, 0:TILE], t[:, ny - TILE :]) for t in (hi, lo))
+            ends[rows, 0:TILE], ends[rows, TILE : 2 * TILE], ends[rows, 2 * TILE :] = hi, lo, hi
+    for r in range(0, nx, per):
+        edges(r)
     late.wait()
     a2[ny : 2 * ny] = a2[0:ny]
     count, top = low.shape[0], nx - high.shape[0]
@@ -227,13 +236,16 @@
         rows_ref[2 * t], rows_ref[2 * t + 1] = value[:, 0:TILE], value[:, TILE:]
 
 
-def main_kernel(nx, edge_ref, var_ref, xhl, a_ref, y_ref, a2):
+def main_kernel(nx, edge_ref, var_ref, xhl, a_ref, lo_ref, y_ref, a2):
     g, ny = y_ref.shape[1], a_ref.shape[1]
     a2[0:ny], a2[ny : 2 * ny] = a_ref[var_ref[0]], a_ref[var_ref[0]]
     step = 4
     for r in range(0, nx, step):
         res = dot(xhl[r * g : (r + step) * g, 0 : 2 * ny], a2[...])
-        y_ref[r : r + step] = res[:, 0 : y_ref.shape[2]].reshape(step, g, y_ref.shape[2])
+        more = dot(xhl[r * g : (r + step) * g, 0:ny], lo_ref[var_ref[0]])
+        at = y_ref.shape[2] - TILE
+        y_ref[r : r + step, :, 0:at] = res[:, 0:at].reshape(step, g, at)
+        y_ref[r : r + step, :, at:] = (res[:, at:] + more).reshape(step, g, TILE)
 
 
 def relay_kernel(edge_ref, var_ref, rows_ref, up_ref, down_ref, one_ref, two_ref):
@@ -325,11 +337,11 @@
     return ok
 
 
-def send_kernel(nx, far, edge_ref, var_ref, yc_ref, ym_ref, one_ref, two_ref, p_ref, *rest):
+def send_kernel(nx, far, edge_ref, var_ref, ym_ref, one_ref, two_ref, p_ref, *rest):
     to_one_ref, to_two_ref, cc_ref, z, y2_ref = rest[:5]
     far_up_ref, far_down_ref, yc, yl, yh, p2 = rest[5:]
     g = yc.shape[1]
-    mains = ym_ref.shape[2]
+    mains = ym_ref.shape[2] - TILE
     ny = mains - TILE
     _, spans = lane_plan(ny)
     n1, n2 = nx >> 1, nx >> 2
@@ -352,7 +364,7 @@
     for r in range(0, nx, step):
         res = dot(z[r * g : (r + step) * g], p2[:, ny : mains + TILE])
         y2_ref[r : r + step] = ym_ref[r : r + step, :, ny:mains] + res[:, 0:TILE].reshape(step, g, TILE)
-        yc[r : r + step] = yc_ref[r : r + step] + res[:, TILE:].reshape(step, g, TILE)
+        yc[r : r + step] = ym_ref[r : r + step, :, mains:] + res[:, TILE:].reshape(step, g, TILE)
     low, high = yl.shape[0], yh.shape[0]
     yl[...] = dot(z[0 : low * g], p2[:, 0:TILE]).reshape(yl.shape)
     yh[...] = dot(z[(nx - high) * g :], p2[:, 0:TILE]).reshape(yh.shape)
@@ -719,7 +731,7 @@
     assert half == TILE and nx % (2 * per) == 0
     far = (nx >> LEVELS) < 2 and gx > 2
     consts = y_constants(ny, gy)
-    main_mat, ehi_mat, elo_mat, s_mat, p_mat = (jnp.asarray(t) for t in consts)
+    main_mat, clo_mat, ehi_mat, elo_mat, s_mat, p_mat = (jnp.asarray(t) for t in consts)
     n1 = nx >> 1
     mains = ny + half
 
@@ -746,16 +758,16 @@
     tile = (g, TILE)
     rows3 = control.reshape(g, nx, ny)
     far_hbm = pl.BlockSpec(memory_space=pltpu.HBM)
-    xhl, yc, one, two, rows = call(
+    xhl, one, two, rows = call(
         partial(first_kernel, nx),
         [
             (pltpu.with_memory_space_constraint(t, pltpu.HBM), far_hbm)
             for t in (rows3, ehi_mat, elo_mat, main_mat)
         ],
-        [((nx * g, 3 * ny), BF), ((nx,) + tile, F32), ((nx // per,) + tile, F32), ((nx // per,) + tile, F32),
+        [((nx * g, 2 * ny), BF), ((nx // per,) + tile, F32), ((nx // per,) + tile, F32),
          ((6,) + tile, F32)],
-        [pltpu.VMEM((nx // per, g, per, ny), F32), pltpu.VMEM((3 * ny, 2 * TILE), BF),
-         pltpu.VMEM((2 * ny, ny), BF), pltpu.VMEM((4, g, ny), F32), pltpu.VMEM((4, g, ny), F32),
+        [pltpu.VMEM((nx // per, g, per, ny), F32), pltpu.VMEM((3 * TILE, TILE), BF),
+         pltpu.VMEM((2 * ny, ny), BF), pltpu.VMEM((nx * g, 3 * TILE), BF), pltpu.VMEM((4, g, ny), F32), pltpu.VMEM((4, g, ny), F32),
          pltpu.SemaphoreType.DMA((nx + 4,))],
     )
     near = swap(rows, "gx", 0)
@@ -763,14 +775,14 @@
     got_two = swap(two, "gy", 1)
     (ym,) = call(
         partial(main_kernel, nx),
-        [(xhl, vmem), (main_mat, vmem)],
-        [((nx, g, mains), F32)],
+        [(xhl, vmem), (main_mat, vmem), (clo_mat, vmem)],
+        [((nx, g, mains + TILE), F32)],
         [pltpu.VMEM((2 * ny, mains + TILE), BF)],
     )
     slots = 2 * n1 + 2
     sent = call(
         partial(send_kernel, nx, far),
-        [(yc, vmem), (ym, vmem), (got_one, vmem), (got_two, vmem), (p_mat, vmem)],
+        [(ym, vmem), (got_one, vmem), (got_two, vmem), (p_mat, vmem)],
         [((6,) + tile, F32), ((6,) + tile, F32), ((slots,) + tile, F32), ((nx * g, 4 * TILE), BF), ((nx,) + tile, F32)]
         + [(tile, F32)] * 2,
         [

time: 28.7 us -> 28 us (0.976)
  Pallas kernels: 12 us -> 11.6 us
  waiting for transfers between devices: 4.66 us -> 4.34 us
    pallas_call x6, Pallas kernels: 12 us -> 11.6 us  [call(): pl.pallas_call(body, out_shape=tuple((jax.ShapeDtypeStruct(*s) for s in o...]
    ppermute x7, waiting for transfers between devices: 4.66 us -> 4.34 us  [swap(): lax.ppermute(value, axis, [p for i in starts for p in ((i, i + step), (i...]
  transfers between devices with their start and end apart: 7 -> 7, of which waited for: 3 -> 3; matrix products, arithmetic and copies ran while one was open for 1% -> 1% of each run, Pallas kernels for 19% -> 20%
where the time goes in v4:
time: 28 us; the launch traced here: 27.9 us
  Pallas kernels  11.6 us (41%)
  starting transfers between devices  11.5 us (41%)
  waiting for transfers between devices  4.34 us (16%)
    pallas_call x6, Pallas kernels, call(): pl.pallas_call(body, out_shape=tuple((jax.ShapeDtypeStruct(*s) for s in o...  11.6 us
    ppermute x7, starting transfers between devices, swap(): lax.ppermute(value, axis, [p for i in starts for p in ((i, i + step), (i...  11.5 us
    ppermute x7, waiting for transfers between devices, swap(): lax.ppermute(value, axis, [p for i in starts for p in ((i, i + step), (i...  4.34 us
  transfers between devices with their start and end apart: 7, of which 3 were waited for; matrix products, arithmetic and copies ran while one was open for 1% of the time, Pallas kernels for 20%

profile of v4, /device:TPU:20, one launch (start us, length us, event | category | flops | bytes accessed | tf_op | source)
XLA Modules:
  0.0 27.9 jit_solution(7538466083078024162)
XLA Ops:
  0.0 0.0 copy-start.1
  0.0 0.0 copy-start.3
  0.0 3.2 %shard_map.82 = (bf16[2048,512]{1,0:T(8,128)(2,1)S(1)}, f32[4,64,128]{2,1,0:T(8,128)S(1)}, f32[4,64,128]{2,1,0:T(8,128)S(1)}, f32[6,64,128]{2,1,0:T(8,128)S(1)}) custom-call(f32[64,32,256]{2,1,0:T(8,128)} %bitcast.2, bf16[3,128,128]{2,1,0:T(8,128)(2,1)} %constant.14.clone.refs_1_, bf16[3,128,128]{2,1,0:T(8,128)(2,1)} %constant.15.clone.refs_2_, ...), custom_call_target="tpu_custom_call" | custom-call | tf_op jit(solution)/shard_map/pallas_call | solution.py:749
  3.2 1.6 %collective-permute-start.2 = (f32[6,64,128]{2,1,0:T(8,128)S(1)}, f32[6,64,128]{2,1,0:T(8,128)S(1)}, u32[]{:S(2)}, u32[]{:S(2)}) collective-permute-start(f32[6,64,128]{2,1,0:T(8,128)S(1)} %get-tuple-element.30), channel_id=1, source_target_pairs={{0,4},{4,0},{8,12},{12,8},{16,20},{20,16},{24,28},{28,24},{1,5},{5... | collective-permute-start | bytes 589832 | tf_op jit(solution)/shard_map/ppermute | solution.py:722
  4.7 0.0 collective-permute-start
  4.7 2.5 %collective-permute-start.1 = (f32[4,64,128]{2,1,0:T(8,128)S(1)}, f32[4,64,128]{2,1,0:T(8,128)S(1)}, u32[]{:S(2)}, u32[]{:S(2)}) collective-permute-start(f32[4,64,128]{2,1,0:T(8,128)S(1)} %get-tuple-element.23), channel_id=1, source_target_pairs={{1,2},{2,1},{5,6},{6,5},{9,10},{10,9},{13,14},{14,13},{17,18},{18,... | collective-permute-start | bytes 393224 | tf_op jit(solution)/shard_map/ppermute | solution.py:722
  7.3 0.0 copy-done.1
  7.3 0.0 copy-done.3
  7.3 0.0 copy-start.2
  7.3 1.5 %shard_map.83.refs_0_ = f32[32,64,512]{2,1,0:T(8,128)S(1)} custom-call(bf16[2048,512]{1,0:T(8,128)(2,1)S(1)} %get-tuple-element.21.refs_0_, bf16[3,256,512]{2,1,0:T(8,128)(2,1)S(1)} %copy-done.1, bf16[3,256,128]{2,1,0:T(8,128)(2,1)S(1)} %copy-done.3), custom_call_target="tpu_custom_call" | custom-call | tf_op jit(solution)/shard_map/pallas_call | solution.py:749
  8.8 0.0 copy-start.4
  8.9 0.0 copy-start
  8.9 0.0 collective-permute-done.refs_1_
  8.9 2.1 %collective-permute-done.1.refs_2_ = f32[4,64,128]{2,1,0:T(8,128)S(1)} collective-permute-done((f32[4,64,128]{2,1,0:T(8,128)S(1)}, f32[4,64,128]{2,1,0:T(8,128)S(1)}, u32[]{:S(2)}, u32[]{:S(2)}) %collective-permute-start.1) | collective-permute-done | bytes 131104 | tf_op jit(solution)/shard_map/ppermute | solution.py:722
  11.0 0.0 copy-done.2
  11.0 1.2 %shard_map.84 = (f32[6,64,128]{2,1,0:T(8,128)S(1)}, f32[6,64,128]{2,1,0:T(8,128)S(1)}, f32[34,64,128]{2,1,0:T(8,128)S(1)}, bf16[2048,512]{1,0:T(8,128)(2,1)S(1)}...) custom-call(f32[32,64,512]{2,1,0:T(8,128)S(1)} %shard_map.83.refs_0_, ...), custom_call_target="tpu_custom_call" | custom-call | tf_op jit(solution)/shard_map/pallas_call | solution.py:749
  12.2 0.6 %collective-permute-start.3 = (f32[6,64,128]{2,1,0:T(8,128)S(1)}, f32[6,64,128]{2,1,0:T(8,128)S(1)}, u32[]{:S(2)}, u32[]{:S(2)}) collective-permute-start(f32[6,64,128]{2,1,0:T(8,128)S(1)} %get-tuple-element.31), channel_id=1, source_target_pairs={{0,4},{4,0},{8,12},{12,8},{16,20},{20,16},{24,28},{28,24},{1,5},{5... | collective-permute-start | bytes 589832 | tf_op jit(solution)/shard_map/ppermute | solution.py:722
  12.8 3.3 %collective-permute-start.4 = (f32[6,64,128]{2,1,0:T(8,128)S(1)}, f32[6,64,128]{2,1,0:T(8,128)S(1)}, u32[]{:S(2)}, u32[]{:S(2)}) collective-permute-start(f32[6,64,128]{2,1,0:T(8,128)S(1)} %get-tuple-element.32), channel_id=1, source_target_pairs={{4,8},{8,4},{12,16},{16,12},{20,24},{24,20},{5,9},{9,5},{13,17},{1... | collective-permute-start | bytes 589832 | tf_op jit(solution)/shard_map/ppermute | solution.py:722
  16.1 0.0 collective-permute-done.2.refs_0_.refs_3_
  16.2 1.6 %collective-permute-start.5 = (f32[5,64,128]{2,1,0:T(8,128)S(1)}, f32[5,64,128]{2,1,0:T(8,128)S(1)}, u32[]{:S(2)}, u32[]{:S(2)}) collective-permute-start(f32[5,64,128]{2,1,0:T(8,128)S(1)} %get-tuple-element.35), channel_id=1, source_target_pairs={{0,8},{8,0},{4,12},{12,4},{16,24},{24,16},{20,28},{28,20},{1,9},{9... | collective-permute-start | bytes 491528 | tf_op jit(solution)/shard_map/ppermute | solution.py:722
  17.8 1.9 %collective-permute-start.6 = (f32[5,64,128]{2,1,0:T(8,128)S(1)}, f32[5,64,128]{2,1,0:T(8,128)S(1)}, u32[]{:S(2)}, u32[]{:S(2)}) collective-permute-start(f32[5,64,128]{2,1,0:T(8,128)S(1)} %get-tuple-element.36), channel_id=1, source_target_pairs={{8,16},{16,8},{12,20},{20,12},{9,17},{17,9},{13,21},{21,13},{10,18... | collective-permute-start | bytes 491528 | tf_op jit(solution)/shard_map/ppermute | solution.py:722
  19.7 0.0 copy-done.4
  19.8 0.1 pad_maximum_fusion.refs_6_.refs_9_
  20.0 0.0 copy-done
  20.0 2.9 %shard_map.85 = (f32[17,64,256]{2,1,0:T(8,128)S(1)}, f32[17,64,256]{2,1,0:T(8,128)S(1)}, f32[38,64,128]{2,1,0:T(8,128)S(1)}) custom-call(f32[32,64,512]{2,1,0:T(8,128)S(1)} %shard_map.83.refs_0_, bf16[2048,512]{1,0:T(8,128)(2,1)S(1)} %get-tuple-element.24.refs_1_, f32[32,64,128]{2,1,0:T(8,128)S(1)} %get-tuple-element.25.refs_2_, ...), custom_call_target="tpu_custom_call" | custom-call | tf_op jit(solution)/shard_map/pallas_call | solution.py:749
  22.8 0.0 collective-permute-done.3.refs_4_
  22.8 0.0 collective-permute-done.4.refs_5_
  22.8 0.2 collective-permute-done.5.refs_6_
  23.1 2.0 %collective-permute-done.6.refs_7_ = f32[5,64,128]{2,1,0:T(8,128)S(1)} collective-permute-done((f32[5,64,128]{2,1,0:T(8,128)S(1)}, f32[5,64,128]{2,1,0:T(8,128)S(1)}, u32[]{:S(2)}, u32[]{:S(2)}) %collective-permute-start.6) | collective-permute-done | bytes 163872 | tf_op jit(solution)/shard_map/ppermute | solution.py:722
  25.0 2.8 %shard_map.87 = f32[64,32,256]{2,1,0:T(8,128)} custom-call(f32[17,64,256]{2,1,0:T(8,128)S(1)} %get-tuple-element.27.refs_0_, f32[17,64,256]{2,1,0:T(8,128)S(1)} %get-tuple-element.28.refs_1_, f32[38,64,128]{2,1,0:T(8,128)S(1)} %get-tuple-element.29.refs_2_, f32[6,64,128]{2,1,0:T(8,128)S(1)} %collective-permute-done.2.refs_0_.refs_3_, ...), custom_call_target="tpu_custom_call" | custom-call | tf_op jit(solution)/shard_map/pallas_call | solution.py:749
  (2 shorter events, 0.1 us)
Async XLA Ops:
  0.0 7.3 %copy-start.1 = (bf16[3,256,512]{2,1,0:T(8,128)(2,1)S(1)}, bf16[3,256,512]{2,1,0:T(8,128)(2,1)}, u32[]{:S(2)}) copy-start(bf16[3,256,512]{2,1,0:T(8,128)(2,1)} %constant.12.clone.refs_3_.refs_1_) | copy-start | bytes 2359300
  0.0 7.3 %copy-start.3 = (bf16[3,256,128]{2,1,0:T(8,128)(2,1)S(1)}, bf16[3,256,128]{2,1,0:T(8,128)(2,1)}, u32[]{:S(2)}) copy-start(bf16[3,256,128]{2,1,0:T(8,128)(2,1)} %constant.13.clone.refs_2_) | copy-start | bytes 589828
  3.2 12.9 %collective-permute-start.2 = (f32[6,64,128]{2,1,0:T(8,128)S(1)}, f32[6,64,128]{2,1,0:T(8,128)S(1)}, u32[]{:S(2)}, u32[]{:S(2)}) collective-permute-start(f32[6,64,128]{2,1,0:T(8,128)S(1)} %get-tuple-element.30), channel_id=1, source_target_pairs={{0,4},{4,0},{8,12},{12,8},{16,20},{20,16},{24,28},{28,24},{1,5},{5... | collective-permute-start | bytes 589832 | tf_op jit(solution)/shard_map/ppermute | solution.py:722
  4.7 4.1 %collective-permute-start = (f32[4,64,128]{2,1,0:T(8,128)S(1)}, f32[4,64,128]{2,1,0:T(8,128)S(1)}, u32[]{:S(2)}, u32[]{:S(2)}) collective-permute-start(f32[4,64,128]{2,1,0:T(8,128)S(1)} %get-tuple-element.22), channel_id=1, source_target_pairs={{0,1},{1,0},{2,3},{3,2},{4,5},{5,4},{6,7},{7,6},{8,9},{9,8},{10,11... | collective-permute-start | bytes 393224 | tf_op jit(solution)/shard_map/ppermute | solution.py:722
  4.7 6.3 %collective-permute-start.1 = (f32[4,64,128]{2,1,0:T(8,128)S(1)}, f32[4,64,128]{2,1,0:T(8,128)S(1)}, u32[]{:S(2)}, u32[]{:S(2)}) collective-permute-start(f32[4,64,128]{2,1,0:T(8,128)S(1)} %get-tuple-element.23), channel_id=1, source_target_pairs={{1,2},{2,1},{5,6},{6,5},{9,10},{10,9},{13,14},{14,13},{17,18},{18,... | collective-permute-start | bytes 393224 | tf_op jit(solution)/shard_map/ppermute | solution.py:722
  7.3 3.7 %copy-start.2 = (bf16[256,512]{1,0:T(8,128)(2,1)S(1)}, bf16[256,512]{1,0:T(8,128)(2,1)}, u32[]{:S(2)}) copy-start(bf16[256,512]{1,0:T(8,128)(2,1)} %constant.17.clone.refs_3_.refs_4_) | copy-start | bytes 786436
  8.8 10.9 %copy-start.4 = (f32[16,32,32]{2,1,0:T(8,128)S(1)}, f32[16,32,32]{2,1,0:T(8,128)}, u32[]{:S(2)}) copy-start(f32[16,32,32]{2,1,0:T(8,128)} %param.9) | copy-start | bytes 196612
  8.9 11.1 %copy-start = (bf16[3,512,256]{2,1,0:T(8,128)(2,1)S(1)}, bf16[3,512,256]{2,1,0:T(8,128)(2,1)}, u32[]{:S(2)}) copy-start(bf16[3,512,256]{2,1,0:T(8,128)(2,1)} %constant.16.clone.refs_5_.refs_8_) | copy-start | bytes 2359300
  12.2 10.6 %collective-permute-start.3 = (f32[6,64,128]{2,1,0:T(8,128)S(1)}, f32[6,64,128]{2,1,0:T(8,128)S(1)}, u32[]{:S(2)}, u32[]{:S(2)}) collective-permute-start(f32[6,64,128]{2,1,0:T(8,128)S(1)} %get-tuple-element.31), channel_id=1, source_target_pairs={{0,4},{4,0},{8,12},{12,8},{16,20},{20,16},{24,28},{28,24},{1,5},{5... | collective-permute-start | bytes 589832 | tf_op jit(solution)/shard_map/ppermute | solution.py:722
  12.8 10.0 %collective-permute-start.4 = (f32[6,64,128]{2,1,0:T(8,128)S(1)}, f32[6,64,128]{2,1,0:T(8,128)S(1)}, u32[]{:S(2)}, u32[]{:S(2)}) collective-permute-start(f32[6,64,128]{2,1,0:T(8,128)S(1)} %get-tuple-element.32), channel_id=1, source_target_pairs={{4,8},{8,4},{12,16},{16,12},{20,24},{24,20},{5,9},{9,5},{13,17},{1... | collective-permute-start | bytes 589832 | tf_op jit(solution)/shard_map/ppermute | solution.py:722
  16.2 6.9 %collective-permute-start.5 = (f32[5,64,128]{2,1,0:T(8,128)S(1)}, f32[5,64,128]{2,1,0:T(8,128)S(1)}, u32[]{:S(2)}, u32[]{:S(2)}) collective-permute-start(f32[5,64,128]{2,1,0:T(8,128)S(1)} %get-tuple-element.35), channel_id=1, source_target_pairs={{0,8},{8,0},{4,12},{12,4},{16,24},{24,16},{20,28},{28,20},{1,9},{9... | collective-permute-start | bytes 491528 | tf_op jit(solution)/shard_map/ppermute | solution.py:722
  17.8 7.2 %collective-permute-start.6 = (f32[5,64,128]{2,1,0:T(8,128)S(1)}, f32[5,64,128]{2,1,0:T(8,128)S(1)}, u32[]{:S(2)}, u32[]{:S(2)}) collective-permute-start(f32[5,64,128]{2,1,0:T(8,128)S(1)} %get-tuple-element.36), channel_id=1, source_target_pairs={{8,16},{16,8},{12,20},{20,12},{9,17},{17,9},{13,21},{21,13},{10,18... | collective-permute-start | bytes 491528 | tf_op jit(solution)/shard_map/ppermute | solution.py:722

commit v5 on v4

--- a/solution.py
+++ b/solution.py
@@ -567,7 +567,36 @@
         store(("m2", "s"), 0, some, weigh_m2(r_ref, "s", [m2.smooth(2, i) for i in some]))
 
 
-def final_kernel(nx, edge_ref, var_ref, vd_ref, vs_ref, w_ref, near, r_one, r_two, f_one, f_two,
+def received_keys():
+    kinds = (("c", "d"), (-1, 0)), (("c", "s"), (0, 1)), (("m2", "d"), (-1, 0)), (("m2", "s"), (0, 1))
+    return [(name, slot) for name, low in kinds for slot in low + ("n-1", "n")]
+
+
+def received_kernel(ny, edge_ref, var_ref, r_one, r_two, r_ref, g_ref):
+    _, spans = lane_plan(ny)
+    s_lanes = smooth_lanes(spans)
+    lev1 = in_span(spans[1])
+
+    def smooth_c(value):
+        return jnp.where(s_lanes, 0.25 * value, 0.0)
+
+    below, above = from_pairs(var_ref[2], r_one, r_two)
+    c_d = [below[3], below[4], above[3], above[4]]
+    c_s = [
+        below[5] + jnp.where(lev1, smooth_c(below[3]), 0.0),
+        smooth_c(below[4]),
+        smooth_c(above[3]),
+        above[5],
+    ]
+    every = list(range(1, LEVELS + 1))
+    tiles = weigh_c(r_ref, spans, "d", every, c_d) + weigh_c(r_ref, spans, "s", every, c_s)
+    tiles += weigh_m2(r_ref, "d", [below[0], below[1], above[0], above[1]])
+    tiles += weigh_m2(r_ref, "s", [below[2], 0.25 * below[1], 0.25 * above[0], above[2]])
+    for j, tile in enumerate(tiles):
+        g_ref[j] = tile
+
+
+def final_kernel(nx, edge_ref, var_ref, vd_ref, vs_ref, w_ref, g_ref, near, r_one, r_two, f_one, f_two,
                  s_ref, r_ref, out_ref, sd, ss, sdeep, zd, zs, zdeep, rows, ot, sem):
     g, ny = ot.shape[1], ot.shape[3]
     _, spans = lane_plan(ny)
@@ -589,30 +618,17 @@
     odd = var_ref[2] == 1
     first_below = [jnp.where(odd, near[t], far_below[1 + t]) for t in range(2)]
     first_above = [jnp.where(odd, far_above[1 + t], near[2 + t]) for t in range(4)]
-    c_d = {-1: below[3], 0: below[4], "n-1": above[3], "n": above[4]}
-    c_s = {
-        0: below[5] + jnp.where(lev1, smooth_c(c_d[-1]), 0.0),
-        1: smooth_c(c_d[0]),
-        "n-1": smooth_c(c_d["n-1"]),
-        "n": above[5],
-    }
-    c_d[-1] = c_d[-1] + far_below[0]
-    c_s[0] = c_s[0] + smooth_c(far_below[0])
-    c_d["n"] = c_d["n"] + far_above[0]
-    c_s["n"] = c_s["n"] + smooth_c(far_above[0])
     fixes = [get_fix(below[2], 0)] + [get_fix(above[2], j) for j in range(2)]
     a_tiles = [first_below[0] + fixes[0][0], first_above[0] + fixes[1][0], first_above[2] + fixes[2][0]]
     b_tiles = [first_below[1] + fixes[0][1], first_above[1] + fixes[1][1], first_above[3] + fixes[2][1]]
     s_tiles = [0.25 * b_tiles[0], 0.25 * b_tiles[1], 0.25 * b_tiles[2] - 1.75 * b_tiles[1]]
-    every = list(range(1, LEVELS + 1))
-    got = {}
-
-    def keep(name, keys, tiles):
-        for key, tile in zip(keys, tiles):
-            got[name, key] = tile
-
-    for kind, tiles in (("d", c_d), ("s", c_s)):
-        keep(("c", kind), list(tiles), weigh_c(r_ref, spans, kind, every, list(tiles.values())))
+    got = {key: g_ref[j] for j, key in enumerate(received_keys())}
+    far_d = weigh_c(r_ref, spans, "d", [LEVELS], [far_below[0], far_above[0]])
+    far_s = weigh_c(r_ref, spans, "s", [LEVELS], [smooth_c(far_below[0]), smooth_c(far_above[0])])
+    got[("c", "d"), -1] += far_d[0]
+    got[("c", "d"), "n"] += far_d[1]
+    got[("c", "s"), 0] += far_s[0]
+    got[("c", "s"), "n"] += far_s[1]
     keys = [-1, "n-1", "n"]
     ta = weigh_tiles(r_ref, band_of(1, "d", "s"), a_tiles)
     tb = weigh_tiles(r_ref, band_of(1, "d", "d"), b_tiles)
@@ -623,9 +639,6 @@
     for j, key in enumerate([0, "n-1", "n"]):
         pairs_into(zs, j, g, [tb[j], jnp.where(lev1, got[("c", "s"), key], 0.0)])
     more_s = dot(zs[...], ss[...])
-    keep(("m2", "d"), [-1, 0, "n-1", "n"], weigh_m2(r_ref, "d", [below[0], below[1], above[0], above[1]]))
-    keep(("m2", "s"), [0, 1, "n-1", "n"],
-         weigh_m2(r_ref, "s", [below[2], 0.25 * below[1], 0.25 * above[0], above[2]]))
 
     def value_of(array, kind, k, i):
         n, low = nx >> k, -1 if kind == "d" else 0
@@ -810,9 +823,12 @@
             pltpu.VMEM((4 * TILE, ny), BF),
         ],
     )
+    (weighed,) = call(
+        partial(received_kernel, ny), [(t, vmem) for t in (got[1], got[2], roots)], [((16,) + tile, F32)], []
+    )
     (out,) = call(
         partial(final_kernel, nx),
-        [(t, vmem) for t in [vd, vs, w] + got + [s_mat, roots]],
+        [(t, vmem) for t in [vd, vs, w, weighed] + got + [s_mat, roots]],
         [((g, nx, ny), F32)],
         [
             pltpu.VMEM((6 * TILE, ny), BF),

time: 28 us -> 27.7 us (0.989)
  waiting for transfers between devices: 4.34 us -> 3.84 us
    ppermute x7, waiting for transfers between devices: 4.34 us -> 3.84 us  [swap(): lax.ppermute(value, axis, [p for i in starts for p in ((i, i + step), (i...]
    pallas_call x6 -> x7, Pallas kernels: 11.6 us -> 11.8 us  [call(): pl.pallas_call(body, out_shape=tuple((jax.ShapeDtypeStruct(*s) for s in o...]
  transfers between devices with their start and end apart: 7 -> 7, of which waited for: 3 -> 2; matrix products, arithmetic and copies ran while one was open for 1% -> 1% of each run, Pallas kernels for 20% -> 22%
where the time goes in v5:
time: 27.7 us; the launch traced here: 27.5 us
  Pallas kernels  11.8 us (43%)
  starting transfers between devices  11.5 us (42%)
  waiting for transfers between devices  3.84 us (14%)
    pallas_call x7, Pallas kernels, call(): pl.pallas_call(body, out_shape=tuple((jax.ShapeDtypeStruct(*s) for s in o...  11.8 us
    ppermute x7, starting transfers between devices, swap(): lax.ppermute(value, axis, [p for i in starts for p in ((i, i + step), (i...  11.5 us
    ppermute x7, waiting for transfers between devices, swap(): lax.ppermute(value, axis, [p for i in starts for p in ((i, i + step), (i...  3.84 us
  transfers between devices with their start and end apart: 7, of which 2 were waited for; matrix products, arithmetic and copies ran while one was open for 1% of the time, Pallas kernels for 22%

profile of v5, /device:TPU:20, one launch (start us, length us, event | category | flops | bytes accessed | tf_op | source)
XLA Modules:
  0.0 27.5 jit_solution(8331327956944091161)
XLA Ops:
  0.0 0.0 copy-start
  0.0 0.0 copy-start.3
  0.0 3.2 %shard_map.82 = (bf16[2048,512]{1,0:T(8,128)(2,1)S(1)}, f32[4,64,128]{2,1,0:T(8,128)S(1)}, f32[4,64,128]{2,1,0:T(8,128)S(1)}, f32[6,64,128]{2,1,0:T(8,128)S(1)}) custom-call(f32[64,32,256]{2,1,0:T(8,128)} %bitcast.2, bf16[3,128,128]{2,1,0:T(8,128)(2,1)} %constant.14.clone.refs_1_, bf16[3,128,128]{2,1,0:T(8,128)(2,1)} %constant.15.clone.refs_2_, ...), custom_call_target="tpu_custom_call" | custom-call | tf_op jit(solution)/shard_map/pallas_call | solution.py:762
  3.2 1.6 %collective-permute-start.4 = (f32[6,64,128]{2,1,0:T(8,128)S(1)}, f32[6,64,128]{2,1,0:T(8,128)S(1)}, u32[]{:S(2)}, u32[]{:S(2)}) collective-permute-start(f32[6,64,128]{2,1,0:T(8,128)S(1)} %get-tuple-element.32), channel_id=1, source_target_pairs={{0,4},{4,0},{8,12},{12,8},{16,20},{20,16},{24,28},{28,24},{1,5},{5... | collective-permute-start | bytes 589832 | tf_op jit(solution)/shard_map/ppermute | solution.py:735
  4.7 0.0 collective-permute-start
  4.7 2.5 %collective-permute-start.1 = (f32[4,64,128]{2,1,0:T(8,128)S(1)}, f32[4,64,128]{2,1,0:T(8,128)S(1)}, u32[]{:S(2)}, u32[]{:S(2)}) collective-permute-start(f32[4,64,128]{2,1,0:T(8,128)S(1)} %get-tuple-element.23), channel_id=1, source_target_pairs={{1,2},{2,1},{5,6},{6,5},{9,10},{10,9},{13,14},{14,13},{17,18},{18,... | collective-permute-start | bytes 393224 | tf_op jit(solution)/shard_map/ppermute | solution.py:735
  7.3 0.0 copy-done
  7.3 0.0 copy-done.3
  7.3 0.0 copy-start.2
  7.3 1.5 %shard_map.83.refs_0_ = f32[32,64,512]{2,1,0:T(8,128)S(1)} custom-call(bf16[2048,512]{1,0:T(8,128)(2,1)S(1)} %get-tuple-element.21.refs_0_, bf16[3,256,512]{2,1,0:T(8,128)(2,1)S(1)} %copy-done, bf16[3,256,128]{2,1,0:T(8,128)(2,1)S(1)} %copy-done.3), custom_call_target="tpu_custom_call" | custom-call | tf_op jit(solution)/shard_map/pallas_call | solution.py:762
  8.8 0.0 copy-start.4
  8.9 0.0 copy-start.1
  8.9 0.0 collective-permute-done.refs_1_
  8.9 2.1 %collective-permute-done.1.refs_2_ = f32[4,64,128]{2,1,0:T(8,128)S(1)} collective-permute-done((f32[4,64,128]{2,1,0:T(8,128)S(1)}, f32[4,64,128]{2,1,0:T(8,128)S(1)}, u32[]{:S(2)}, u32[]{:S(2)}) %collective-permute-start.1) | collective-permute-done | bytes 131104 | tf_op jit(solution)/shard_map/ppermute | solution.py:735
  11.0 0.0 copy-done.2
  11.0 1.2 %shard_map.84 = (f32[6,64,128]{2,1,0:T(8,128)S(1)}, f32[6,64,128]{2,1,0:T(8,128)S(1)}, f32[34,64,128]{2,1,0:T(8,128)S(1)}, bf16[2048,512]{1,0:T(8,128)(2,1)S(1)}...) custom-call(f32[32,64,512]{2,1,0:T(8,128)S(1)} %shard_map.83.refs_0_, ...), custom_call_target="tpu_custom_call" | custom-call | tf_op jit(solution)/shard_map/pallas_call | solution.py:762
  12.2 0.6 %collective-permute-start.2 = (f32[6,64,128]{2,1,0:T(8,128)S(1)}, f32[6,64,128]{2,1,0:T(8,128)S(1)}, u32[]{:S(2)}, u32[]{:S(2)}) collective-permute-start(f32[6,64,128]{2,1,0:T(8,128)S(1)} %get-tuple-element.30), channel_id=1, source_target_pairs={{0,4},{4,0},{8,12},{12,8},{16,20},{20,16},{24,28},{28,24},{1,5},{5... | collective-permute-start | bytes 589832 | tf_op jit(solution)/shard_map/ppermute | solution.py:735
  12.8 3.3 %collective-permute-start.3 = (f32[6,64,128]{2,1,0:T(8,128)S(1)}, f32[6,64,128]{2,1,0:T(8,128)S(1)}, u32[]{:S(2)}, u32[]{:S(2)}) collective-permute-start(f32[6,64,128]{2,1,0:T(8,128)S(1)} %get-tuple-element.31), channel_id=1, source_target_pairs={{4,8},{8,4},{12,16},{16,12},{20,24},{24,20},{5,9},{9,5},{13,17},{1... | collective-permute-start | bytes 589832 | tf_op jit(solution)/shard_map/ppermute | solution.py:735
  16.1 0.0 collective-permute-done.4.refs_0_.refs_4_
  16.2 1.6 %collective-permute-start.5 = (f32[5,64,128]{2,1,0:T(8,128)S(1)}, f32[5,64,128]{2,1,0:T(8,128)S(1)}, u32[]{:S(2)}, u32[]{:S(2)}) collective-permute-start(f32[5,64,128]{2,1,0:T(8,128)S(1)} %get-tuple-element.35), channel_id=1, source_target_pairs={{0,8},{8,0},{4,12},{12,4},{16,24},{24,16},{20,28},{28,20},{1,9},{9... | collective-permute-start | bytes 491528 | tf_op jit(solution)/shard_map/ppermute | solution.py:735
  17.8 1.9 %collective-permute-start.6 = (f32[5,64,128]{2,1,0:T(8,128)S(1)}, f32[5,64,128]{2,1,0:T(8,128)S(1)}, u32[]{:S(2)}, u32[]{:S(2)}) collective-permute-start(f32[5,64,128]{2,1,0:T(8,128)S(1)} %get-tuple-element.36), channel_id=1, source_target_pairs={{8,16},{16,8},{12,20},{20,12},{9,17},{17,9},{13,21},{21,13},{10,18... | collective-permute-start | bytes 491528 | tf_op jit(solution)/shard_map/ppermute | solution.py:735
  19.7 0.0 copy-done.4
  19.8 0.1 pad_maximum_fusion.refs_6_.refs_2_.refs_10_
  20.0 0.0 copy-done.1
  20.0 2.9 %shard_map.85 = (f32[17,64,256]{2,1,0:T(8,128)S(1)}, f32[17,64,256]{2,1,0:T(8,128)S(1)}, f32[38,64,128]{2,1,0:T(8,128)S(1)}) custom-call(f32[32,64,512]{2,1,0:T(8,128)S(1)} %shard_map.83.refs_0_, bf16[2048,512]{1,0:T(8,128)(2,1)S(1)} %get-tuple-element.24.refs_1_, f32[32,64,128]{2,1,0:T(8,128)S(1)} %get-tuple-element.25.refs_2_, ...), custom_call_target="tpu_custom_call" | custom-call | tf_op jit(solution)/shard_map/pallas_call | solution.py:762
  22.8 0.0 collective-permute-done.2.refs_0_.refs_5_
  22.8 0.0 collective-permute-done.3.refs_1_.refs_6_
  22.8 0.5 %shard_map.86.refs_3_ = f32[16,64,128]{2,1,0:T(8,128)S(1)} custom-call(f32[6,64,128]{2,1,0:T(8,128)S(1)} %collective-permute-done.2.refs_0_.refs_5_, f32[6,64,128]{2,1,0:T(8,128)S(1)} %collective-permute-done.3.refs_1_.refs_6_, bf16[16,32,96]{2,1,0:T(8,128)(2,1)S(1)} %pad_maximum_fusion.refs_6_.refs_2_.refs_10_), custom_call_target="tpu_custom_call" | custom-call | tf_op jit(solution)/shard_map/pallas_call | solution.py:762
  23.3 0.0 collective-permute-done.5.refs_7_
  23.3 1.7 %collective-permute-done.6.refs_8_ = f32[5,64,128]{2,1,0:T(8,128)S(1)} collective-permute-done((f32[5,64,128]{2,1,0:T(8,128)S(1)}, f32[5,64,128]{2,1,0:T(8,128)S(1)}, u32[]{:S(2)}, u32[]{:S(2)}) %collective-permute-start.6) | collective-permute-done | bytes 163872 | tf_op jit(solution)/shard_map/ppermute | solution.py:735
  25.0 2.5 %shard_map.88 = f32[64,32,256]{2,1,0:T(8,128)} custom-call(f32[17,64,256]{2,1,0:T(8,128)S(1)} %get-tuple-element.27.refs_0_, f32[17,64,256]{2,1,0:T(8,128)S(1)} %get-tuple-element.28.refs_1_, f32[38,64,128]{2,1,0:T(8,128)S(1)} %get-tuple-element.29.refs_2_, f32[16,64,128]{2,1,0:T(8,128)S(1)} %shard_map.86.refs_3_, ...), custom_call_target="tpu_custom_call" | custom-call | tf_op jit(solution)/shard_map/pallas_call | solution.py:762
  (2 shorter events, 0.1 us)
Async XLA Ops:
  0.0 7.3 %copy-start = (bf16[3,256,512]{2,1,0:T(8,128)(2,1)S(1)}, bf16[3,256,512]{2,1,0:T(8,128)(2,1)}, u32[]{:S(2)}) copy-start(bf16[3,256,512]{2,1,0:T(8,128)(2,1)} %constant.12.clone.refs_3_.refs_1_) | copy-start | bytes 2359300
  0.0 7.3 %copy-start.3 = (bf16[3,256,128]{2,1,0:T(8,128)(2,1)S(1)}, bf16[3,256,128]{2,1,0:T(8,128)(2,1)}, u32[]{:S(2)}) copy-start(bf16[3,256,128]{2,1,0:T(8,128)(2,1)} %constant.13.clone.refs_2_) | copy-start | bytes 589828
  3.2 12.9 %collective-permute-start.4 = (f32[6,64,128]{2,1,0:T(8,128)S(1)}, f32[6,64,128]{2,1,0:T(8,128)S(1)}, u32[]{:S(2)}, u32[]{:S(2)}) collective-permute-start(f32[6,64,128]{2,1,0:T(8,128)S(1)} %get-tuple-element.32), channel_id=1, source_target_pairs={{0,4},{4,0},{8,12},{12,8},{16,20},{20,16},{24,28},{28,24},{1,5},{5... | collective-permute-start | bytes 589832 | tf_op jit(solution)/shard_map/ppermute | solution.py:735
  4.7 4.1 %collective-permute-start = (f32[4,64,128]{2,1,0:T(8,128)S(1)}, f32[4,64,128]{2,1,0:T(8,128)S(1)}, u32[]{:S(2)}, u32[]{:S(2)}) collective-permute-start(f32[4,64,128]{2,1,0:T(8,128)S(1)} %get-tuple-element.22), channel_id=1, source_target_pairs={{0,1},{1,0},{2,3},{3,2},{4,5},{5,4},{6,7},{7,6},{8,9},{9,8},{10,11... | collective-permute-start | bytes 393224 | tf_op jit(solution)/shard_map/ppermute | solution.py:735
  4.7 6.3 %collective-permute-start.1 = (f32[4,64,128]{2,1,0:T(8,128)S(1)}, f32[4,64,128]{2,1,0:T(8,128)S(1)}, u32[]{:S(2)}, u32[]{:S(2)}) collective-permute-start(f32[4,64,128]{2,1,0:T(8,128)S(1)} %get-tuple-element.23), channel_id=1, source_target_pairs={{1,2},{2,1},{5,6},{6,5},{9,10},{10,9},{13,14},{14,13},{17,18},{18,... | collective-permute-start | bytes 393224 | tf_op jit(solution)/shard_map/ppermute | solution.py:735
  7.3 3.7 %copy-start.2 = (bf16[256,512]{1,0:T(8,128)(2,1)S(1)}, bf16[256,512]{1,0:T(8,128)(2,1)}, u32[]{:S(2)}) copy-start(bf16[256,512]{1,0:T(8,128)(2,1)} %constant.17.clone.refs_3_.refs_4_) | copy-start | bytes 786436
  8.8 10.9 %copy-start.4 = (f32[16,32,32]{2,1,0:T(8,128)S(1)}, f32[16,32,32]{2,1,0:T(8,128)}, u32[]{:S(2)}) copy-start(f32[16,32,32]{2,1,0:T(8,128)} %param.9) | copy-start | bytes 196612
  8.9 11.1 %copy-start.1 = (bf16[3,512,256]{2,1,0:T(8,128)(2,1)S(1)}, bf16[3,512,256]{2,1,0:T(8,128)(2,1)}, u32[]{:S(2)}) copy-start(bf16[3,512,256]{2,1,0:T(8,128)(2,1)} %constant.16.clone.refs_5_.refs_9_) | copy-start | bytes 2359300
  12.2 10.6 %collective-permute-start.2 = (f32[6,64,128]{2,1,0:T(8,128)S(1)}, f32[6,64,128]{2,1,0:T(8,128)S(1)}, u32[]{:S(2)}, u32[]{:S(2)}) collective-permute-start(f32[6,64,128]{2,1,0:T(8,128)S(1)} %get-tuple-element.30), channel_id=1, source_target_pairs={{0,4},{4,0},{8,12},{12,8},{16,20},{20,16},{24,28},{28,24},{1,5},{5... | collective-permute-start | bytes 589832 | tf_op jit(solution)/shard_map/ppermute | solution.py:735
  12.8 10.0 %collective-permute-start.3 = (f32[6,64,128]{2,1,0:T(8,128)S(1)}, f32[6,64,128]{2,1,0:T(8,128)S(1)}, u32[]{:S(2)}, u32[]{:S(2)}) collective-permute-start(f32[6,64,128]{2,1,0:T(8,128)S(1)} %get-tuple-element.31), channel_id=1, source_target_pairs={{4,8},{8,4},{12,16},{16,12},{20,24},{24,20},{5,9},{9,5},{13,17},{1... | collective-permute-start | bytes 589832 | tf_op jit(solution)/shard_map/ppermute | solution.py:735
  16.2 7.1 %collective-permute-start.5 = (f32[5,64,128]{2,1,0:T(8,128)S(1)}, f32[5,64,128]{2,1,0:T(8,128)S(1)}, u32[]{:S(2)}, u32[]{:S(2)}) collective-permute-start(f32[5,64,128]{2,1,0:T(8,128)S(1)} %get-tuple-element.35), channel_id=1, source_target_pairs={{0,8},{8,0},{4,12},{12,4},{16,24},{24,16},{20,28},{28,20},{1,9},{9... | collective-permute-start | bytes 491528 | tf_op jit(solution)/shard_map/ppermute | solution.py:735
  17.8 7.2 %collective-permute-start.6 = (f32[5,64,128]{2,1,0:T(8,128)S(1)}, f32[5,64,128]{2,1,0:T(8,128)S(1)}, u32[]{:S(2)}, u32[]{:S(2)}) collective-permute-start(f32[5,64,128]{2,1,0:T(8,128)S(1)} %get-tuple-element.36), channel_id=1, source_target_pairs={{8,16},{16,8},{12,20},{20,12},{9,17},{17,9},{13,21},{21,13},{10,18... | collective-permute-start | bytes 491528 | tf_op jit(solution)/shard_map/ppermute | solution.py:735
